TPU v7x, 32 devices: a whole 2x2x4 slice. The times are simulated.
32 devices in a mesh: rep: 2 (over core), mp: 16 (over z, y, x).
Axes of the slice: x: 2, y: 2, z: 4, core: 2. Of those that a mesh axis runs over, the one named last changes fastest.
Arguments:
- lookup_block: int32 [2, 2048, 16, 4], P(None, ('rep', 'mp')), may hold values from 0 to 9
- lookup_offset: int32 [2, 2048, 16, 4], P(None, ('rep', 'mp')), may hold values from 0 to 63
- interaction_grad: bfloat16 [2, 2048, 16, 16], P(None, ('rep', 'mp')), may hold values from -4 to 4
- table: bfloat16 [49152, 256], P('mp'), may hold values from -0.3125 to 0.3125
- adagrad_state: float32 [49152], P('mp'), may hold values from 0.05 to 2
- touched_blocks: int32 [16, 10], P('mp'), may hold values from 0 to 47, as said below
- dither: int32 [16, 640, 256], P('mp'), may hold values from 0 to 32767
Outputs:
- new_table: bfloat16 [49152, 256], P('mp')
- new_state: float32 [49152], P('mp')
Inputs may be any that keep to these rules, and one draw needn't show every extreme that they name: `touched_blocks`: each row names 10 different row blocks.
All inputs are finite; a program needn't handle non-finite values.
Results may differ from a plain program's by a relative error of at most 0.00055.
The roundings to bfloat16 on the way count: a program that leaves them out, or rounds other values in their place, can miss the bound.
Values may be sent and summed in bfloat16 or wider, within the bound.
A program may use at most 128 MiB of HBM per device.

v0:
```python
import jax
import jax.numpy as jnp
from jax import lax
from jax.sharding import PartitionSpec as P

BLOCK = 64


LEARN_RATE = 0.1
POOL_DECAY = 0.5
DITHER_UNIT = 2.0 ** (-15)
SMALLEST = 2.0 ** (-14)


def dither_round(weights, dither_bits):
    magnitude = jnp.maximum(jnp.abs(weights), SMALLEST)
    spacing = jnp.exp2(jnp.floor(jnp.log2(magnitude)) - 7.0)
    grid_level = jnp.floor(weights / spacing + dither_bits.astype(jnp.float32) * DITHER_UNIT)
    return (grid_level * spacing).astype(jnp.bfloat16)


def adagrad_rows(slab_rows, grad_rows, state_rows, dither_bits):
    state_next = state_rows + jnp.mean(grad_rows * grad_rows, axis=-1)
    moved = (
        slab_rows.astype(jnp.float32)
        - LEARN_RATE * grad_rows / (jnp.sqrt(state_next) + 1e-08)[:, None]
    )
    return (dither_round(moved, dither_bits), state_next)


def hit_counts(lookup_rows, slab_size):
    column = lax.broadcasted_iota(jnp.int32, (1, slab_size), 1)
    counted = jnp.zeros((lookup_rows.shape[0], slab_size), jnp.bfloat16)
    for lookup in range(lookup_rows.shape[1]):
        counted = counted + (lookup_rows[:, lookup : lookup + 1] == column).astype(jnp.bfloat16)
    return counted


def pairwise(pooled_rows, cotangent):
    forward = jnp.einsum("bfg,bge->bfe", cotangent, pooled_rows, preferred_element_type=jnp.float32)
    backward = jnp.einsum(
        "bgf,bge->bfe", cotangent, pooled_rows, preferred_element_type=jnp.float32
    )
    return (forward + backward + POOL_DECAY * pooled_rows.astype(jnp.float32)).astype(jnp.bfloat16)


def per_device(
    lookup_block, lookup_offset, interaction_grad, table, adagrad_state, touched_blocks, dither
):
    micro_count, sample_count, feature_count, bag_count = lookup_block.shape
    groups = lax.axis_size("mp")
    row_count, emb_width = table.shape
    touch_count = touched_blocks.shape[1]
    slab_size = touch_count * BLOCK
    owner_samples = groups * sample_count
    lookup_rows = lookup_block * BLOCK + lookup_offset
    owner_rows = lax.all_to_all(lookup_rows, "mp", split_axis=2, concat_axis=1, tiled=True)
    owner_rows = owner_rows.reshape(micro_count, owner_samples, bag_count)
    table_blocks = table.reshape(row_count // BLOCK, BLOCK, emb_width)
    slab_table = table_blocks[touched_blocks[0]].reshape(slab_size, emb_width)
    counted = [hit_counts(owner_rows[micro_index], slab_size) for micro_index in range(micro_count)]
    pooled_rows = [
        jnp.dot(hits, slab_table, preferred_element_type=jnp.float32).astype(jnp.bfloat16)
        for hits in counted
    ]
    returned = []
    outgoing = jnp.stack(pooled_rows).reshape(micro_count, groups, sample_count, 1, emb_width)
    arrived = lax.all_to_all(outgoing, "mp", split_axis=1, concat_axis=3, tiled=True)
    sample_pooled = arrived.reshape(micro_count * sample_count, feature_count, emb_width)
    cot_rows = interaction_grad.reshape(micro_count * sample_count, feature_count, feature_count)
    grad_rows = pairwise(sample_pooled, cot_rows)
    grad_rows = grad_rows.reshape(micro_count, 1, sample_count, feature_count, emb_width)
    sent_back = lax.all_to_all(grad_rows, "mp", split_axis=3, concat_axis=1, tiled=True)
    sent_back = sent_back.reshape(micro_count, owner_samples, emb_width)
    returned = [sent_back[micro_index] for micro_index in range(micro_count)]
    slab_grad = jnp.zeros((slab_size, emb_width), jnp.float32)
    for micro_index in range(micro_count):
        slab_grad = slab_grad + jnp.einsum(
            "sr,se->re",
            counted[micro_index],
            returned[micro_index],
            preferred_element_type=jnp.float32,
        )
    state_slab = adagrad_state.reshape(row_count // BLOCK, BLOCK)[touched_blocks[0]].reshape(
        slab_size
    )
    summed_grad = lax.psum(slab_grad, "rep")
    new_rows, state_next = adagrad_rows(slab_table, summed_grad, state_slab, dither[0])
    updated_blocks = table_blocks.at[touched_blocks[0]].set(
        new_rows.reshape(touch_count, BLOCK, emb_width)
    )
    state_blocks = adagrad_state.reshape(row_count // BLOCK, BLOCK)
    updated_state = state_blocks.at[touched_blocks[0]].set(state_next.reshape(touch_count, BLOCK))
    return (updated_blocks.reshape(row_count, emb_width), updated_state.reshape(row_count))


def solution(mesh):
    return jax.shard_map(
        per_device,
        mesh=mesh,
        in_specs=(
            P(None, ("rep", "mp"), None, None),
            P(None, ("rep", "mp"), None, None),
            P(None, ("rep", "mp"), None, None),
            P("mp", None),
            P("mp"),
            P("mp", None),
            P("mp", None, None),
        ),
        out_specs=(P("mp", None), P("mp")),
        check_vma=False,
    )
```

profile of v0, /device:TPU:0, one launch (start us, length us, event | category | flops | bytes accessed | tf_op | source)
XLA Modules:
  0.0 124.7 jit_solution(17753280693400444190)
XLA Ops:
  7.2 1.5 %copy.46 = bf16[3072,256]{1,0:T(8,128)(2,1)S(1)} copy(bf16[3072,256]{1,0:T(8,128)(2,1)} %param.10) | data formatting | bytes 3145728
  8.7 0.7 reshape.142
  9.4 8.3 %all-to-all-start = ((s32[16,1,512]{2,1,0:T(1,128)}), s32[16,1,512]{2,1,0:T(1,128)S(1)}, u32[]{:S(2)}, u32[]{:S(2)}) async-start(s32[16,1,512]{2,1,0:T(1,128)} %reshape.142), calls=%async_computation | async-start | bytes 65536 | tf_op jit(solution)/shard_map/all_to_all | solution.py:57
  17.8 0.6 gather_fusion
  18.4 6.8 %all-to-all-done = s32[16,1,512]{2,1,0:T(1,128)S(1)} async-done(((s32[16,1,512]{2,1,0:T(1,128)}), s32[16,1,512]{2,1,0:T(1,128)S(1)}, u32[]{:S(2)}, u32[]{:S(2)}) %all-to-all-start) | async-done | bytes 32800 | tf_op jit(solution)/shard_map/all_to_all | solution.py:57
  25.2 0.5 broadcast.49
  25.7 0.7 reduce
  26.8 1.8 %convolution_convert_fusion.1 = bf16[1024,256]{1,0:T(8,128)(2,1)S(1)} fusion(bf16[640,256]{1,0:T(8,128)(2,1)S(1)} %bitcast.83, s32[1024]{0:T(1024)S(1)} %bitcast.91, s32[1024]{0:T(1024)S(1)} %bitcast.93, s32[1024]{0:T(1024)S(1)} %bitcast.95, s32[1024]{0:T(1024)S(1)} %bitcast.89), kind=kOutput, calls=%fused_computation.29 | convolution fusion | flops 346292224 | bytes 868352 | tf_op jit(solution)/shard_map/dot_general | solution.py:63
  28.6 1.8 %convolution_convert_fusion = bf16[1024,256]{1,0:T(8,128)(2,1)S(1)} fusion(bf16[640,256]{1,0:T(8,128)(2,1)S(1)} %bitcast.84, s32[1024]{0:T(1024)S(1)} %bitcast.99, s32[1024]{0:T(1024)S(1)} %bitcast.101, s32[1024]{0:T(1024)S(1)} %bitcast.103, s32[1024]{0:T(1024)S(1)} %bitcast.97), kind=kOutput, calls=%fused_computation.28 | convolution fusion | flops 346292224 | bytes 868352 | tf_op jit(solution)/shard_map/dot_general | solution.py:63
  30.3 1.1 pad_maximum_fusion
  31.4 3.7 %all-to-all-start.1 = ((bf16[2,16,64,1,256]{4,2,3,0,1:T(8,128)(2,1)}), bf16[2,16,64,1,256]{4,2,3,0,1:T(8,128)(2,1)S(1)}, u32[]{:S(2)}, u32[]{:S(2)}) async-start(bf16[2,16,64,1,256]{4,2,3,0,1:T(8,128)(2,1)} %pad_maximum_fusion), calls=%async_computation.1 | async-start | bytes 2097152 | tf_op jit(solution)/shard_map/all_to_all | solution.py:68
  35.1 1.4 %copy.30 = bf16[2,64,16,16]{2,3,1,0:T(8,128)(2,1)S(1)} copy(bf16[2,64,16,16]{1,3,2,0:T(8,128)(2,1)} %param.9) | data formatting | bytes 131072 | tf_op jit(solution)/shard_map/reshape | solution.py:70
  36.5 21.7 %all-to-all-done.1 = bf16[2,16,64,1,256]{4,2,3,0,1:T(8,128)(2,1)S(1)} async-done(((bf16[2,16,64,1,256]{4,2,3,0,1:T(8,128)(2,1)}), bf16[2,16,64,1,256]{4,2,3,0,1:T(8,128)(2,1)S(1)}, u32[]{:S(2)}, u32[]{:S(2)}) %all-to-all-start.1) | async-done | bytes 1048608 | tf_op jit(solution)/shard_map/all_to_all | solution.py:68
  58.3 0.6 copy.24
  60.2 30.6 %all_to_all.45 = bf16[2,1,64,16,256]{4,2,0,1,3:T(8,128)(2,1)S(1)} all-to-all(bf16[2,1,64,16,256]{4,2,0,1,3:T(8,128)(2,1)S(1)} %copy.28), channel_id=1, replica_groups=mesh['rep'=2,'mp'=16] {'mp'}, dimensions={3} | all-to-all | bytes 2097152 | tf_op jit(solution)/shard_map/all_to_all | solution.py:73
  91.0 1.7 %fusion.15 = f32[640,256]{1,0:T(8,128)S(1)} fusion(bf16[1024,256]{1,0:T(8,128)(2,1)S(1)} %bitcast.86, s32[1024]{0:T(1024)S(1)} %bitcast.92, s32[1024]{0:T(1024)S(1)} %bitcast.94, s32[1024]{0:T(1024)S(1)} %bitcast.96, s32[1024]{0:T(1024)S(1)} %bitcast.90), kind=kOutput, calls=%fused_computation.31 | convolution fusion | flops 346030080 | bytes 1196032 | tf_op jit(solution)/shard_map/sr,se->re/dot_general | solution.py:78
  92.8 2.5 %convolution_add_fusion = f32[640,256]{1,0:T(8,128)} fusion(f32[640,256]{1,0:T(8,128)S(1)} %fusion.15, bf16[1024,256]{1,0:T(8,128)(2,1)S(1)} %bitcast.85, s32[1024]{0:T(1024)S(1)} %bitcast.100, s32[1024]{0:T(1024)S(1)} %bitcast.102, s32[1024]{0:T(1024)S(1)} %bitcast.104, s32[1024]{0:T(1024)S(1)} %bitcast.98), kind=kOutput, calls=%fused_computation.30 | convolution fusion | flops 346193920 | bytes 1851392 | tf_op jit(solution)/shard_map/sr,se->re/dot_general | solution.py:78
  95.4 0.6 gather_fusion.1
  96.0 16.5 %all-reduce.2.cloned.1.call-done = f32[640,256]{1,0:T(8,128)} async-done(((f32[640,256]{1,0:T(8,128)}), f32[640,256]{1,0:T(8,128)}) %all-reduce.2.cloned.1.call-update) | async-done | bytes 655376 | tf_op jit(solution)/shard_map/psum | solution.py:87
  112.5 1.3 %multiply_reduce_fusion = f32[640]{0:T(1024)S(1)} fusion(f32[640,256]{1,0:T(8,128)} %all-reduce.2.cloned.1.call-done), kind=kLoop, calls=%fused_computation.38 | loop fusion | flops 327040 | bytes 657920 | tf_op jit(solution)/shard_map/reduce_sum | solution.py:23
  113.8 1.6 %fusion.22 = bf16[640,256]{1,0:T(8,128)(2,1)S(1)} fusion(s32[1,640,256]{2,1,0:T(8,128)S(1)} %copy-done.1, f32[640,256]{1,0:T(8,128)} %all-reduce.2.cloned.1.call-done, f32[640]{0:T(1024)S(1)} %get-tuple-element.15, bf16[10,64,256]{2,1,0:T(8,128)(2,1)S(1)} %gather_fusion), kind=kLoop, calls=%fused_computation.37 | loop fusion | flops 2785280 | bytes 1968640 | tf_op jit(solution)/shard_map/convert_element_type | solution.py:19
  115.4 1.0 scatter_fusion
  116.5 0.6 scatter_custom_fusion.1
  117.2 0.7 reshape.107
  (35 shorter events, 2.2 us)
Async XLA Ops:
  7.2 1.5 %copy-start.3 = (s32[2,64,16,4]{1,3,2,0:T(4,128)S(1)}, s32[2,64,16,4]{1,3,2,0:T(4,128)}, u32[]{:S(2)}) copy-start(s32[2,64,16,4]{1,3,2,0:T(4,128)} %param.7) | copy-start | bytes 98308
  7.2 1.5 %copy-start.2 = (s32[2,64,16,4]{1,3,2,0:T(4,128)S(1)}, s32[2,64,16,4]{1,3,2,0:T(4,128)}, u32[]{:S(2)}) copy-start(s32[2,64,16,4]{1,3,2,0:T(4,128)} %param.8) | copy-start | bytes 98308
  7.2 10.6 %copy-start.5 = (s32[1,10]{1,0:T(1,128)S(1)}, s32[1,10]{1,0:T(1,128)}, u32[]{:S(2)}) copy-start(s32[1,10]{1,0:T(1,128)} %param.12) | copy-start | bytes 124
  9.4 15.8 %all-to-all-start = ((s32[16,1,512]{2,1,0:T(1,128)}), s32[16,1,512]{2,1,0:T(1,128)S(1)}, u32[]{:S(2)}, u32[]{:S(2)}) async-start(s32[16,1,512]{2,1,0:T(1,128)} %reshape.142), calls=%async_computation | async-start | bytes 65536 | tf_op jit(solution)/shard_map/all_to_all | solution.py:57
  31.4 26.9 %all-to-all-start.1 = ((bf16[2,16,64,1,256]{4,2,3,0,1:T(8,128)(2,1)}), bf16[2,16,64,1,256]{4,2,3,0,1:T(8,128)(2,1)S(1)}, u32[]{:S(2)}, u32[]{:S(2)}) async-start(bf16[2,16,64,1,256]{4,2,3,0,1:T(8,128)(2,1)} %pad_maximum_fusion), calls=%async_computation.1 | async-start | bytes 2097152 | tf_op jit(solution)/shard_map/all_to_all | solution.py:68
  35.1 77.4 %all-reduce.2.cloned.1.call-start = ((), (), s32[]{:S(2)}) async-start(), calls=%async_computation.3 | async-start | bytes 1310720 | tf_op jit(solution)/shard_map/psum | solution.py:87
  92.7 2.5 %copy-start.4 = (f32[3072]{0:T(1024)S(1)}, f32[3072]{0:T(1024)}, u32[]{:S(2)}) copy-start(f32[3072]{0:T(1024)} %param.11) | copy-start | bytes 36868
  92.7 21.0 %copy-start.1 = (s32[1,640,256]{2,1,0:T(8,128)S(1)}, s32[1,640,256]{2,1,0:T(8,128)}, u32[]{:S(2)}) copy-start(s32[1,640,256]{2,1,0:T(8,128)} %param.13) | copy-start | bytes 1966084
  116.5 1.4 %copy-start = (bf16[48,64,256]{2,1,0:T(8,128)(2,1)}, bf16[48,64,256]{2,1,0:T(8,128)(2,1)S(1)}, u32[]{:S(2)}) copy-start(bf16[48,64,256]{2,1,0:T(8,128)(2,1)S(1)} %scatter_fusion) | copy-start | bytes 4718596
Sparse Core Ops, SparseCore 0:
  95.4 17.0 all-reduce.1
where the time goes:
time: 125 us
  waiting for transfers between devices  45 us (36%)
  blocking collectives  30.6 us (24%)
  between operations  14.3 us (11%)
  starting transfers between devices  12 us (10%)
  matrix products  8.71 us (7%)
  local copies, waits for them, and re-layouts  8.62 us (7%)
  other arithmetic  5.37 us (4%)
    all_to_all x1, blocking collectives, per_device(): lax.all_to_all(grad_rows, 'mp', split_axis=3, concat_axis=1, tiled=True)  30.6 us
    all_to_all x1, waiting for transfers between devices, per_device(): lax.all_to_all(outgoing, 'mp', split_axis=1, concat_axis=3, tiled=True)  21.7 us
    psum x1, waiting for transfers between devices, per_device(): summed_grad = lax.psum(slab_grad, 'rep')  16.5 us
    all_to_all x1, starting transfers between devices, per_device(): lax.all_to_all(lookup_rows, 'mp', split_axis=2, concat_axis=1, tiled=True)  8.34 us
    all_to_all x1, waiting for transfers between devices, per_device(): lax.all_to_all(lookup_rows, 'mp', split_axis=2, concat_axis=1, tiled=True)  6.79 us
    dot_general x2, matrix products, per_device(): jnp.einsum('sr,se->re', counted[micro_index], returned[micro_index], pref...  4.17 us
    all_to_all x1, starting transfers between devices, per_device(): lax.all_to_all(outgoing, 'mp', split_axis=1, concat_axis=3, tiled=True)  3.66 us
    dot_general x2, matrix products, per_device(): jnp.dot(hits, slab_table, preferred_element_type=jnp.float32)  3.58 us
  transfers between devices with their start and end apart: 3, of which 3 were waited for; matrix products, arithmetic and copies ran while one was open for 2% of the time, Pallas kernels for 0%

commit v1 on v0

v1 whole, which is shorter than its diff:
```python
import functools

import jax
import jax.numpy as jnp
from jax import lax
from jax.experimental import pallas as pl
from jax.experimental.pallas import tpu as pltpu
from jax.sharding import PartitionSpec as P

BLOCK = 64
LEARN_RATE = 0.1
POOL_DECAY = 0.5
DITHER_UNIT = 2.0 ** (-15)
SMALLEST = 2.0 ** (-14)
MESH = pl.DeviceIdType.MESH


def dither_round(weights, dither_bits):
    magnitude = jnp.maximum(jnp.abs(weights), SMALLEST)
    spacing = jnp.exp2(jnp.floor(jnp.log2(magnitude)) - 7.0)
    grid_level = jnp.floor(weights / spacing + dither_bits.astype(jnp.float32) * DITHER_UNIT)
    return (grid_level * spacing).astype(jnp.bfloat16)


def step_kernel(
    n,
    rows_ref,
    w_ref,
    slab_ref,
    state_ref,
    dither_ref,
    out_ref,
    state_out_ref,
    rows_all,
    w_other,
    slab_t,
    pooled_out,
    pooled_in,
    grad_out,
    grad_in,
    total,
    squares,
    rows_new,
    small_sem,
    rows_send,
    rows_recv,
    pooled_send,
    pooled_recv,
    grad_send,
    grad_recv,
):
    me = lax.axis_index("mp")
    half = lax.axis_index("rep")
    bags, samples = rows_ref.shape[1:]
    slab_size = slab_ref.shape[0]
    width = slab_t.shape[0]
    columns = pl.ds(pl.multiple_of(half * width, width), width)

    def at(peer):
        return {"device_id": (half, peer), "device_id_type": MESH}

    partner = {"device_id": (1 - half, me), "device_id_type": MESH}

    def peer_of(step):
        return lax.rem(me + step, n)

    def each_peer(body):
        def run(step, carry):
            body(peer_of(step))
            return carry

        lax.fori_loop(1, n, run, 0)

    barrier = pltpu.get_barrier_semaphore()
    each_peer(lambda peer: pl.semaphore_signal(barrier, inc=1, **at(peer)))
    pl.semaphore_signal(barrier, inc=1, **partner)
    pl.semaphore_wait(barrier, n)

    def rows_copy(peer, slot):
        return pltpu.make_async_remote_copy(
            rows_ref.at[peer],
            rows_all.at[half, slot],
            rows_send.at[peer],
            rows_recv.at[slot],
            **at(peer),
        )

    each_peer(lambda peer: rows_copy(peer, me).start())
    own_rows = pltpu.make_async_copy(rows_ref.at[me], rows_all.at[half, me], small_sem.at[0])
    own_rows.start()
    w_copy = pltpu.make_async_remote_copy(
        w_ref, w_other, small_sem.at[1], small_sem.at[2], **partner
    )
    w_copy.start()
    slab_t[...] = slab_ref[:, columns].astype(jnp.float32).T.astype(jnp.bfloat16)
    total[...] = jnp.zeros_like(total)
    own_rows.wait()
    each_peer(lambda peer: rows_copy(peer, peer).wait_recv())
    swap = pltpu.make_async_remote_copy(
        rows_all.at[half], rows_all.at[half], small_sem.at[3], small_sem.at[4], **partner
    )
    swap.start()

    slab_row = lax.broadcasted_iota(jnp.int32, (slab_size, samples), 0)

    def hits(rep, peer):
        block = rows_all[rep, peer]
        counted = jnp.zeros((slab_size, samples), jnp.float32)
        for lookup in range(bags):
            counted = counted + jnp.where(slab_row == block[lookup : lookup + 1, :], 1.0, 0.0)
        return counted.astype(jnp.bfloat16)

    def pooled_copy(part, peer, slot):
        return pltpu.make_async_remote_copy(
            pooled_out.at[part, peer],
            pooled_in.at[part, slot],
            pooled_send.at[part, peer],
            pooled_recv.at[part, slot],
            **at(peer),
        )

    def grad_copy(part, peer, slot):
        return pltpu.make_async_remote_copy(
            grad_out.at[part, peer],
            grad_in.at[part, slot],
            grad_send.at[part, peer],
            grad_recv.at[part, slot],
            **at(peer),
        )

    def pool(part, rep):
        def pooled(peer):
            return jnp.dot(
                slab_t[...], hits(rep, peer), preferred_element_type=jnp.float32
            ).astype(jnp.bfloat16)

        def send(peer):
            pooled_out[part, peer] = pooled(peer)
            pooled_copy(part, peer, me).start()

        each_peer(send)
        pooled_in[part, me] = pooled(me)

    def interact(part, weights):
        each_peer(lambda peer: pooled_copy(part, peer, peer).wait_recv())

        def mixed(feature):
            def add(other, carry):
                weight = weights[pl.ds(feature * n + other, 1), :]
                return carry + weight * pooled_in[part, other].astype(jnp.float32)

            zero = jnp.zeros((width, samples), jnp.float32)
            return lax.fori_loop(0, n, add, zero, unroll=4).astype(jnp.bfloat16)

        def send(peer):
            grad_out[part, peer] = mixed(peer)
            grad_copy(part, peer, me).start()

        each_peer(send)
        grad_in[part, me] = mixed(me)

    def collect(part, rep):
        def add(peer):
            total[...] += lax.dot_general(
                hits(rep, peer),
                grad_in[part, peer],
                (((1,), (1,)), ((), ())),
                preferred_element_type=jnp.float32,
            )

        def take(peer):
            grad_copy(part, peer, peer).wait_recv()
            add(peer)

        add(me)
        each_peer(take)

    pool(0, half)
    swap.wait_recv()
    pool(1, 1 - half)
    interact(0, w_ref)
    w_copy.wait_recv()
    interact(1, w_other)
    collect(0, half)
    collect(1, 1 - half)

    grad = total[...]
    squares[0] = jnp.sum((grad * grad).T, axis=0, keepdims=True)
    square_copy = pltpu.make_async_remote_copy(
        squares.at[0], squares.at[1], small_sem.at[5], small_sem.at[6], **partner
    )
    square_copy.start()
    square_copy.wait_recv()
    first = jnp.where(half == 0, squares[0], squares[1])
    second = jnp.where(half == 0, squares[1], squares[0])
    state_next = state_ref[...] + (first + second) / (2.0 * width)
    state_out_ref[...] = state_next
    divisor = jnp.broadcast_to(jnp.sqrt(state_next) + 1e-08, (width, slab_size)).T
    moved = slab_ref[:, columns].astype(jnp.float32) - LEARN_RATE * grad / divisor
    rows_new[0] = dither_round(moved, dither_ref[:, columns])
    new_copy = pltpu.make_async_remote_copy(
        rows_new.at[0], rows_new.at[1], small_sem.at[7], small_sem.at[8], **partner
    )
    new_copy.start()
    out_ref[:, columns] = rows_new[0]

    each_peer(lambda peer: rows_copy(peer, peer).wait_send())
    for part in range(2):
        each_peer(lambda peer: pooled_copy(part, peer, peer).wait_send())
        each_peer(lambda peer: grad_copy(part, peer, peer).wait_send())
    w_copy.wait_send()
    swap.wait_send()
    square_copy.wait_send()
    new_copy.wait()
    out_ref[:, pl.ds(pl.multiple_of((1 - half) * width, width), width)] = rows_new[1]


def fused_step(n, rows, weights, slab, state_row, dither):
    bags, samples = rows.shape[1:]
    slab_size, emb_width = slab.shape
    width = emb_width // 2
    dma = pltpu.SemaphoreType.DMA
    block = (2, n, width, samples)
    vmem = pl.BlockSpec(memory_space=pltpu.VMEM)
    return pl.pallas_call(
        functools.partial(step_kernel, n),
        out_shape=(
            jax.ShapeDtypeStruct((slab_size, emb_width), jnp.bfloat16),
            jax.ShapeDtypeStruct((1, slab_size), jnp.float32),
        ),
        in_specs=[vmem] * 5,
        out_specs=(vmem, vmem),
        scratch_shapes=[
            pltpu.VMEM((2, n, bags, samples), jnp.int32),
            pltpu.VMEM(weights.shape, jnp.float32),
            pltpu.VMEM((width, slab_size), jnp.bfloat16),
            pltpu.VMEM(block, jnp.bfloat16),
            pltpu.VMEM(block, jnp.bfloat16),
            pltpu.VMEM(block, jnp.bfloat16),
            pltpu.VMEM(block, jnp.bfloat16),
            pltpu.VMEM((slab_size, width), jnp.float32),
            pltpu.VMEM((2, 1, slab_size), jnp.float32),
            pltpu.VMEM((2, slab_size, width), jnp.bfloat16),
            dma((9,)),
            dma((n,)),
            dma((n,)),
            dma((2, n)),
            dma((2, n)),
            dma((2, n)),
            dma((2, n)),
        ],
        compiler_params=pltpu.CompilerParams(collective_id=0, has_side_effects=True),
        name="fused_step",
    )(rows, weights, slab, state_row, dither)


def per_device(
    lookup_block, lookup_offset, interaction_grad, table, adagrad_state, touched_blocks, dither
):
    micro_count, sample_count, feature_count, bag_count = lookup_block.shape
    n = lax.axis_size("mp")
    samples = micro_count * sample_count
    row_count, emb_width = table.shape
    touch_count = touched_blocks.shape[1]
    slab_size = touch_count * BLOCK
    rows = (lookup_block * BLOCK + lookup_offset).reshape(samples, feature_count * bag_count)
    rows = rows.T.reshape(feature_count, bag_count, samples)
    cot = interaction_grad.reshape(samples, feature_count, feature_count).astype(jnp.float32)
    weights = cot + jnp.swapaxes(cot, 1, 2) + POOL_DECAY * jnp.eye(feature_count)
    weights = weights.reshape(samples, feature_count * feature_count).T
    table_blocks = table.reshape(row_count // BLOCK, BLOCK, emb_width)
    slab = table_blocks[touched_blocks[0]].reshape(slab_size, emb_width)
    state_blocks = adagrad_state.reshape(row_count // BLOCK, BLOCK)
    state_row = state_blocks[touched_blocks[0]].reshape(1, slab_size)
    new_rows, state_next = fused_step(n, rows, weights, slab, state_row, dither[0])
    updated_blocks = table_blocks.at[touched_blocks[0]].set(
        new_rows.reshape(touch_count, BLOCK, emb_width)
    )
    updated_state = state_blocks.at[touched_blocks[0]].set(state_next.reshape(touch_count, BLOCK))
    return (updated_blocks.reshape(row_count, emb_width), updated_state.reshape(row_count))


def solution(mesh):
    return jax.shard_map(
        per_device,
        mesh=mesh,
        in_specs=(
            P(None, ("rep", "mp"), None, None),
            P(None, ("rep", "mp"), None, None),
            P(None, ("rep", "mp"), None, None),
            P("mp", None),
            P("mp"),
            P("mp", None),
            P("mp", None, None),
        ),
        out_specs=(P("mp", None), P("mp")),
        check_vma=False,
    )
```

time: 125 us -> 77.9 us (0.62)
  the two profiles are of different devices: /device:TPU:0 before, /device:TPU:15 now
where the time goes in v1:
time: 77.9 us; the launch traced here: 77.6 us
  Pallas kernels  67 us (86%)
  local copies, waits for them, and re-layouts  8.45 us (11%)
  other arithmetic  1.47 us (2%)
    pallas_call x1, Pallas kernels, fused_step(): pl.pallas_call(functools.partial(step_kernel, n), out_shape=(jax.ShapeDty...  67 us
    scatter x1, local copies, waits for them, and re-layouts, per_device(): table_blocks.at[touched_blocks[0]]  1.89 us

profile of v1, /device:TPU:15, one launch (start us, length us, event | category | flops | bytes accessed | tf_op | source)
XLA Modules:
  0.0 77.6 jit_solution(4274132863802561015)
XLA Ops:
  0.6 0.0 copy-start.3
  0.6 0.0 copy-start.2
  0.7 0.0 copy-start.1
  0.7 0.0 copy-start.4
  0.7 0.0 copy-start.5
  0.7 1.5 %copy.17 = bf16[3072,256]{1,0:T(8,128)(2,1)S(1)} copy(bf16[3072,256]{1,0:T(8,128)(2,1)} %param.10) | data formatting | bytes 3145728
  2.2 0.0 copy-done.4
  2.2 0.1 reshape.81
  2.3 0.6 gather_fusion.1
  2.8 0.7 reshape.82.state_ref
  3.5 0.0 copy-done.3
  3.5 0.1 copy.10
  3.6 0.7 reshape.77
  4.3 0.1 copy.11
  4.4 0.2 reshape.87
  4.6 0.7 fusion
  5.4 1.3 %gather_fusion = bf16[10,64,256]{2,1,0:T(8,128)(2,1)} fusion(bf16[48,64,256]{2,1,0:T(8,128)(2,1)S(1)} %bitcast.25, s32[1024]{0:T(1024)S(1)} %pad_clamp_fusion), kind=kCustom, calls=%fused_computation | custom fusion | bytes 655400 | tf_op jit(solution)/shard_map/gather | solution.py:272
  6.7 67.0 %fused_step.1 = (bf16[640,256]{1,0:T(8,128)(2,1)}, f32[1,640]{1,0:T(1,128)}) custom-call(s32[16,4,128]{2,1,0:T(4,128)} %bitcast.32, f32[256,128]{1,0:T(8,128)} %bitcast.30, bf16[640,256]{1,0:T(8,128)(2,1)} %bitcast.28, f32[1,640]{1,0:T(1,128)} %reshape.82.state_ref, s32[640,256]{1,0:T(8,128)} %bitcast.29), custom_call_target="tpu_custom_call" | custom-call | tf_op jit(solution)/shard_map/fused_step/pallas_call | solution.py:225
  73.6 1.9 %scatter_fusion = bf16[48,64,256]{2,1,0:T(8,128)(2,1)S(1)} fusion(bf16[48,64,256]{2,1,0:T(8,128)(2,1)S(1)} %bitcast.26, s32[10]{0:T(128)S(1)} %fusion.2, bf16[10,64,256]{2,1,0:T(8,128)(2,1)} %bitcast.31), kind=kCustom, calls=%fused_computation.2 | custom fusion | bytes 983080 | tf_op jit(solution)/shard_map/scatter | solution.py:276
  75.5 0.0 copy-start
  75.6 0.7 reduce
  76.2 0.1 reshape.116
  76.3 0.6 scatter_fusion.1
  77.0 0.7 reshape.86
  (8 shorter events, 0.0 us)
Async XLA Ops:
  0.6 2.9 %copy-start.3 = (s32[2,64,16,4]{1,3,2,0:T(4,128)S(1)}, s32[2,64,16,4]{1,3,2,0:T(4,128)}, u32[]{:S(2)}) copy-start(s32[2,64,16,4]{1,3,2,0:T(4,128)} %param.7) | copy-start | bytes 98308
  0.6 2.9 %copy-start.2 = (s32[2,64,16,4]{1,3,2,0:T(4,128)S(1)}, s32[2,64,16,4]{1,3,2,0:T(4,128)}, u32[]{:S(2)}) copy-start(s32[2,64,16,4]{1,3,2,0:T(4,128)} %param.8) | copy-start | bytes 98308
  0.7 3.7 %copy-start.1 = (bf16[2,64,16,16]{1,3,2,0:T(8,128)(2,1)S(1)}, bf16[2,64,16,16]{1,3,2,0:T(8,128)(2,1)}, u32[]{:S(2)}) copy-start(bf16[2,64,16,16]{1,3,2,0:T(8,128)(2,1)} %param.9) | copy-start | bytes 196612
  0.7 1.5 %copy-start.4 = (f32[3072]{0:T(1024)S(1)}, f32[3072]{0:T(1024)}, u32[]{:S(2)}) copy-start(f32[3072]{0:T(1024)} %param.11) | copy-start | bytes 36868
  0.7 1.5 %copy-start.5 = (s32[1,10]{1,0:T(1,128)S(1)}, s32[1,10]{1,0:T(1,128)}, u32[]{:S(2)}) copy-start(s32[1,10]{1,0:T(1,128)} %param.12) | copy-start | bytes 124
  75.5 2.1 %copy-start = (bf16[48,64,256]{2,1,0:T(8,128)(2,1)}, bf16[48,64,256]{2,1,0:T(8,128)(2,1)S(1)}, u32[]{:S(2)}) copy-start(bf16[48,64,256]{2,1,0:T(8,128)(2,1)S(1)} %scatter_fusion) | copy-start | bytes 4718596

commit v2 on v1

v2 whole, which is shorter than its diff:
```python
import functools

import jax
import jax.numpy as jnp
from jax import lax
from jax.experimental import pallas as pl
from jax.experimental.pallas import tpu as pltpu
from jax.sharding import PartitionSpec as P

BLOCK = 64
LEARN_RATE = 0.1
POOL_DECAY = 0.5
DITHER_UNIT = 2.0 ** (-15)
SMALLEST = 2.0 ** (-14)
KEEP_BYTES = 8 << 20
MESH = pl.DeviceIdType.MESH


def dither_round(weights, dither_bits):
    magnitude = jnp.maximum(jnp.abs(weights), SMALLEST)
    spacing = jnp.exp2(jnp.floor(jnp.log2(magnitude)) - 7.0)
    grid_level = jnp.floor(weights / spacing + dither_bits.astype(jnp.float32) * DITHER_UNIT)
    return (grid_level * spacing).astype(jnp.bfloat16)


def step_kernel(
    n,
    rows_ref,
    w_ref,
    slab_ref,
    state_ref,
    dither_ref,
    out_ref,
    state_out_ref,
    near,
    far,
    w_other,
    slab_t,
    pooled_out,
    pooled_in,
    grad_out,
    grad_in,
    kept,
    total,
    squares,
    rows_new,
    small_sem,
    rows_send,
    near_recv,
    far_recv,
    pooled_send,
    pooled_recv,
    grad_send,
    grad_recv,
):
    me = lax.axis_index("mp")
    rep = lax.axis_index("rep")
    m = n // 2
    group = me // m
    local = lax.rem(me, m)
    mirror = lax.rem(me + m, n)
    bags, samples = rows_ref.shape[2:]
    slab_size = slab_ref.shape[0]
    width = slab_t.shape[1]
    keeps = kept.shape[1] == m
    columns = pl.ds(pl.multiple_of(rep * width, width), width)

    def at(peer):
        return {"device_id": (rep, peer), "device_id_type": MESH}

    partner = {"device_id": (1 - rep, me), "device_id_type": MESH}

    def each(first, body):
        def run(step, carry):
            body(lax.rem(local + step, m))
            return carry

        lax.fori_loop(first, m, run, 0)

    def near_at(j):
        return group * m + j

    def far_at(j):
        return (1 - group) * m + j

    barrier = pltpu.get_barrier_semaphore()
    each(1, lambda j: pl.semaphore_signal(barrier, inc=1, **at(near_at(j))))
    each(0, lambda j: pl.semaphore_signal(barrier, inc=1, **at(far_at(j))))
    pl.semaphore_signal(barrier, inc=1, **partner)
    slab_t[0] = slab_ref[:, columns].astype(jnp.float32).T.astype(jnp.bfloat16)
    own_rows = pltpu.make_async_copy(rows_ref.at[local], near.at[rep, local], small_sem.at[0])
    own_rows.start()
    total[...] = jnp.zeros_like(total)
    pl.semaphore_wait(barrier, n)

    def near_copy(j, slot):
        return pltpu.make_async_remote_copy(
            rows_ref.at[j],
            near.at[rep, slot],
            rows_send.at[0, j],
            near_recv.at[slot],
            **at(near_at(j)),
        )

    def far_copy(j, slot):
        return pltpu.make_async_remote_copy(
            rows_ref.at[j, 1 - group],
            far.at[rep, slot],
            rows_send.at[1, j],
            far_recv.at[slot],
            **at(far_at(j)),
        )

    each(1, lambda j: near_copy(j, local).start())
    slab_copy = pltpu.make_async_remote_copy(
        slab_t.at[0], slab_t.at[1], small_sem.at[9], small_sem.at[10], **at(mirror)
    )
    slab_copy.start()
    w_copy = pltpu.make_async_remote_copy(
        w_ref, w_other, small_sem.at[1], small_sem.at[2], **partner
    )
    w_copy.start()
    each(0, lambda j: far_copy(j, local).start())
    own_rows.wait()
    each(1, lambda j: near_copy(j, j).wait_recv())
    swap_near = pltpu.make_async_remote_copy(
        near.at[rep], near.at[rep], small_sem.at[3], small_sem.at[4], **partner
    )
    swap_near.start()

    offset_in_block = lax.broadcasted_iota(jnp.int32, (BLOCK, samples), 0)
    offset_in_block = offset_in_block.astype(jnp.float32).astype(jnp.bfloat16)
    one = jnp.ones((BLOCK, samples), jnp.bfloat16)

    def hits(rows):
        blocks = []
        block_of, offset_of = rows // BLOCK, lax.rem(rows, BLOCK)
        for block in range(slab_size // BLOCK):
            wanted = jnp.where(block_of == block, offset_of, -1).astype(jnp.float32)
            counted = jnp.zeros((BLOCK, samples), jnp.bfloat16)
            for lookup in range(bags):
                row = jnp.broadcast_to(wanted[lookup : lookup + 1, :], (BLOCK, samples))
                same = row.astype(jnp.bfloat16) == offset_in_block
                counted = counted + jnp.where(same, one, jnp.zeros_like(one))
            blocks.append(counted)
        return jnp.concatenate(blocks, axis=0)

    def pooled_copy(part, which, j, slot):
        return pltpu.make_async_remote_copy(
            pooled_out.at[part, which, j],
            pooled_in.at[part, slot],
            pooled_send.at[part, which, j],
            pooled_recv.at[part, slot],
            **at(near_at(j)),
        )

    def grad_copy(part, peer, slot):
        return pltpu.make_async_remote_copy(
            grad_out.at[part, peer],
            grad_in.at[part, slot],
            grad_send.at[part, peer],
            grad_recv.at[part, slot],
            **at(peer),
        )

    def pool(part, replica, which):
        table = group if which == 0 else 1 - group
        feature = me if which == 0 else mirror

        def pooled(j):
            counted = hits(near[replica, j, table])
            if which == 0 and keeps:
                kept[part, j] = counted
            return jnp.dot(slab_t[which], counted, preferred_element_type=jnp.float32).astype(
                jnp.bfloat16
            )

        def send(j):
            pooled_out[part, which, j] = pooled(j)
            pooled_copy(part, which, j, feature).start()

        each(1, send)
        pooled_in[part, feature] = pooled(local)

    def interact(part, weights):
        def arrive(j):
            pooled_copy(part, 0, j, near_at(j)).wait_recv()
            pooled_copy(part, 1, j, far_at(j)).wait_recv()

        each(1, arrive)

        def mixed(feature):
            def add(other, carry):
                weight = weights[pl.ds(feature * n + other, 1), :]
                return carry + weight * pooled_in[part, other].astype(jnp.float32)

            zero = jnp.zeros((width, samples), jnp.float32)
            return lax.fori_loop(0, n, add, zero, unroll=4).astype(jnp.bfloat16)

        def send(peer):
            grad_out[part, peer] = mixed(peer)
            grad_copy(part, peer, me).start()

        each(0, lambda j: send(far_at(j)))
        each(1, lambda j: send(near_at(j)))
        grad_in[part, me] = mixed(me)

    def collect(part, replica):
        def add(peer, counted):
            total[...] += lax.dot_general(
                counted,
                grad_in[part, peer],
                (((1,), (1,)), ((), ())),
                preferred_element_type=jnp.float32,
            )

        def near_hits(j):
            return kept[part, j] if keeps else hits(near[replica, j, group])

        def take_near(j):
            grad_copy(part, near_at(j), near_at(j)).wait_recv()
            add(near_at(j), near_hits(j))

        def take_far(j):
            counted = hits(far[replica, j])
            grad_copy(part, far_at(j), far_at(j)).wait_recv()
            add(far_at(j), counted)

        add(me, near_hits(local))
        each(1, take_near)
        each(0, take_far)

    pool(0, rep, 0)
    swap_near.wait_recv()
    pool(1, 1 - rep, 0)
    each(0, lambda j: far_copy(j, j).wait_recv())
    swap_far = pltpu.make_async_remote_copy(
        far.at[rep], far.at[rep], small_sem.at[11], small_sem.at[12], **partner
    )
    swap_far.start()
    slab_copy.wait_recv()
    pool(0, rep, 1)
    pool(1, 1 - rep, 1)
    interact(0, w_ref)
    w_copy.wait_recv()
    interact(1, w_other)
    collect(0, rep)
    swap_far.wait_recv()
    collect(1, 1 - rep)

    grad = total[...]
    squares[0] = jnp.sum((grad * grad).T, axis=0, keepdims=True)
    square_copy = pltpu.make_async_remote_copy(
        squares.at[0], squares.at[1], small_sem.at[5], small_sem.at[6], **partner
    )
    square_copy.start()
    square_copy.wait_recv()
    first = jnp.where(rep == 0, squares[0], squares[1])
    second = jnp.where(rep == 0, squares[1], squares[0])
    state_next = state_ref[...] + (first + second) / (2.0 * width)
    state_out_ref[...] = state_next
    divisor = jnp.broadcast_to(jnp.sqrt(state_next) + 1e-08, (width, slab_size)).T
    moved = slab_ref[:, columns].astype(jnp.float32) - LEARN_RATE * grad / divisor
    rows_new[0] = dither_round(moved, dither_ref[:, columns])
    new_copy = pltpu.make_async_remote_copy(
        rows_new.at[0], rows_new.at[1], small_sem.at[7], small_sem.at[8], **partner
    )
    new_copy.start()
    out_ref[:, columns] = rows_new[0]

    each(1, lambda j: near_copy(j, j).wait_send())
    each(0, lambda j: far_copy(j, j).wait_send())
    for part in range(2):
        for which in range(2):
            each(1, lambda j: pooled_copy(part, which, j, j).wait_send())
        each(1, lambda j: grad_copy(part, near_at(j), me).wait_send())
        each(0, lambda j: grad_copy(part, far_at(j), me).wait_send())
    slab_copy.wait_send()
    w_copy.wait_send()
    swap_near.wait_send()
    swap_far.wait_send()
    square_copy.wait_send()
    new_copy.wait()
    out_ref[:, pl.ds(pl.multiple_of((1 - rep) * width, width), width)] = rows_new[1]


def fused_step(n, rows, weights, slab, state_row, dither):
    bags, samples = rows.shape[2:]
    slab_size, emb_width = slab.shape
    width = emb_width // 2
    m = n // 2
    keep = m if 4 * m * slab_size * samples <= KEEP_BYTES else 1
    dma = pltpu.SemaphoreType.DMA
    block = (2, n, width, samples)
    vmem = pl.BlockSpec(memory_space=pltpu.VMEM)
    return pl.pallas_call(
        functools.partial(step_kernel, n),
        out_shape=(
            jax.ShapeDtypeStruct((slab_size, emb_width), jnp.bfloat16),
            jax.ShapeDtypeStruct((1, slab_size), jnp.float32),
        ),
        in_specs=[vmem] * 5,
        out_specs=(vmem, vmem),
        scratch_shapes=[
            pltpu.VMEM((2, m, 2, bags, samples), jnp.int32),
            pltpu.VMEM((2, m, bags, samples), jnp.int32),
            pltpu.VMEM(weights.shape, jnp.float32),
            pltpu.VMEM((2, width, slab_size), jnp.bfloat16),
            pltpu.VMEM((2, 2, m, width, samples), jnp.bfloat16),
            pltpu.VMEM(block, jnp.bfloat16),
            pltpu.VMEM(block, jnp.bfloat16),
            pltpu.VMEM(block, jnp.bfloat16),
            pltpu.VMEM((2, keep, slab_size, samples), jnp.bfloat16),
            pltpu.VMEM((slab_size, width), jnp.float32),
            pltpu.VMEM((2, 1, slab_size), jnp.float32),
            pltpu.VMEM((2, slab_size, width), jnp.bfloat16),
            dma((13,)),
            dma((2, m)),
            dma((m,)),
            dma((m,)),
            dma((2, 2, m)),
            dma((2, n)),
            dma((2, n)),
            dma((2, n)),
        ],
        compiler_params=pltpu.CompilerParams(collective_id=0, has_side_effects=True),
        name="fused_step",
    )(rows, weights, slab, state_row, dither)


def per_device(
    lookup_block, lookup_offset, interaction_grad, table, adagrad_state, touched_blocks, dither
):
    micro_count, sample_count, feature_count, bag_count = lookup_block.shape
    n = lax.axis_size("mp")
    samples = micro_count * sample_count
    row_count, emb_width = table.shape
    touch_count = touched_blocks.shape[1]
    slab_size = touch_count * BLOCK
    rows = (lookup_block * BLOCK + lookup_offset).reshape(samples, feature_count * bag_count)
    rows = rows.T.reshape(2, feature_count // 2, bag_count, samples).swapaxes(0, 1)
    cot = interaction_grad.reshape(samples, feature_count, feature_count).astype(jnp.float32)
    weights = cot + jnp.swapaxes(cot, 1, 2) + POOL_DECAY * jnp.eye(feature_count)
    weights = weights.reshape(samples, feature_count * feature_count).T
    table_blocks = table.reshape(row_count // BLOCK, BLOCK, emb_width)
    slab = table_blocks[touched_blocks[0]].reshape(slab_size, emb_width)
    state_blocks = adagrad_state.reshape(row_count // BLOCK, BLOCK)
    state_row = state_blocks[touched_blocks[0]].reshape(1, slab_size)
    new_rows, state_next = fused_step(n, rows, weights, slab, state_row, dither[0])
    updated_blocks = table_blocks.at[touched_blocks[0]].set(
        new_rows.reshape(touch_count, BLOCK, emb_width)
    )
    updated_state = state_blocks.at[touched_blocks[0]].set(state_next.reshape(touch_count, BLOCK))
    return (updated_blocks.reshape(row_count, emb_width), updated_state.reshape(row_count))


def solution(mesh):
    return jax.shard_map(
        per_device,
        mesh=mesh,
        in_specs=(
            P(None, ("rep", "mp"), None, None),
            P(None, ("rep", "mp"), None, None),
            P(None, ("rep", "mp"), None, None),
            P("mp", None),
            P("mp"),
            P("mp", None),
            P("mp", None, None),
        ),
        out_specs=(P("mp", None), P("mp")),
        check_vma=False,
    )
```

time: 77.9 us -> 65.3 us (0.84)
  the two profiles are of different devices: /device:TPU:15 before, /device:TPU:0 now
where the time goes in v2:
time: 65.3 us; the launch traced here: 65 us
  Pallas kernels  54.3 us (83%)
  local copies, waits for them, and re-layouts  8.46 us (13%)
  other arithmetic  1.47 us (2%)
  between operations  0.75 us (1%)
    pallas_call x1, Pallas kernels, fused_step(): pl.pallas_call(functools.partial(step_kernel, n), out_shape=(jax.ShapeDty...  54.3 us
    scatter x1, local copies, waits for them, and re-layouts, per_device(): table_blocks.at[touched_blocks[0]]  1.89 us
    unnamed x13, local copies, waits for them, and re-layouts  1.52 us
    gather x1, local copies, waits for them, and re-layouts, per_device(): slab = table_blocks[touched_blocks[0]].reshape(slab_size, emb_width)  1.31 us

profile of v2, /device:TPU:0, one launch (start us, length us, event | category | flops | bytes accessed | tf_op | source)
XLA Modules:
  0.0 65.0 jit_solution(842232934026126295)
XLA Ops:
  0.6 0.0 copy-start.3
  0.6 0.0 copy-start.2
  0.7 0.0 copy-start.1
  0.7 0.0 copy-start.4
  0.7 0.0 copy-start.5
  0.7 1.5 %copy.20 = bf16[3072,256]{1,0:T(8,128)(2,1)S(1)} copy(bf16[3072,256]{1,0:T(8,128)(2,1)} %param.10) | data formatting | bytes 3145728
  2.2 0.0 copy-done.4
  2.2 0.1 reshape.81
  2.3 0.6 gather_fusion.1
  2.8 0.7 %reshape.82.state_ref = f32[1,640]{1,0:T(1,128)} reshape(f32[10,64]{1,0:T(8,128)S(1)} %gather_fusion.1) | data formatting | bytes 5120 | tf_op jit(solution)/shard_map/reshape | solution.py:348
  3.5 0.1 copy.10
  3.6 0.1 reshape.77
  3.7 0.6 copy.16
  4.3 0.1 copy.12
  4.5 0.2 reshape.87
  4.6 0.7 %fusion = f32[128,16,16]{0,2,1:T(8,128)} fusion(f32[128,16,16]{0,2,1:T(8,128)S(1)} %reshape.87, f32[16,16]{1,0:T(8,128)S(1)} %fusion.1), kind=kLoop, calls=%fused_computation.5 | loop fusion | flops 65536 | bytes 263168 | tf_op jit(solution)/shard_map/add | solution.py:343
  5.4 1.3 %gather_fusion = bf16[10,64,256]{2,1,0:T(8,128)(2,1)} fusion(bf16[48,64,256]{2,1,0:T(8,128)(2,1)S(1)} %bitcast.28, s32[1024]{0:T(1024)S(1)} %pad_clamp_fusion), kind=kCustom, calls=%fused_computation | custom fusion | bytes 655400 | tf_op jit(solution)/shard_map/gather | solution.py:346
  6.7 54.3 %fused_step.1 = (bf16[640,256]{1,0:T(8,128)(2,1)}, f32[1,640]{1,0:T(1,128)}) custom-call(s32[8,2,4,128]{3,2,1,0:T(4,128)} %bitcast.35, f32[256,128]{1,0:T(8,128)} %bitcast.33, bf16[640,256]{1,0:T(8,128)(2,1)} %bitcast.31, f32[1,640]{1,0:T(1,128)} %reshape.82.state_ref, s32[640,256]{1,0:T(8,128)} %bitcast.32), custom_call_target="tpu_custom_call" | custom-call | tf_op jit(solution)/shard_map/fused_step/pallas_call | solution.py:296
  61.0 1.9 %scatter_fusion = bf16[48,64,256]{2,1,0:T(8,128)(2,1)S(1)} fusion(bf16[48,64,256]{2,1,0:T(8,128)(2,1)S(1)} %bitcast.29, s32[10]{0:T(128)S(1)} %fusion.2, bf16[10,64,256]{2,1,0:T(8,128)(2,1)} %bitcast.34), kind=kCustom, calls=%fused_computation.2 | custom fusion | bytes 983080 | tf_op jit(solution)/shard_map/scatter | solution.py:350
  62.9 0.0 copy-start
  63.0 0.7 %reduce = f32[640]{0:T(1024)S(1)} reduce(f32[1,640]{1,0:T(1,128)} %get-tuple-element.5, f32[]{:T(128)} %constant.12), dimensions={0}, to_apply=%get-tuple-element.5.reduce_sub_computation | reduce | bytes 5124 | tf_op jit(solution)/shard_map/fused_step/pallas_call | solution.py:296
  63.6 0.1 reshape.116
  63.7 0.6 scatter_fusion.1
  64.4 0.7 %reshape.86 = f32[3072]{0:T(1024)} reshape(f32[48,64]{1,0:T(8,128)S(1)} %scatter_fusion.1) | data formatting | bytes 24576 | tf_op jit(solution)/shard_map/reshape | solution.py:354
  (9 shorter events, 0.0 us)
Async XLA Ops:
  0.6 2.9 %copy-start.3 = (s32[2,64,16,4]{1,3,2,0:T(4,128)S(1)}, s32[2,64,16,4]{1,3,2,0:T(4,128)}, u32[]{:S(2)}) copy-start(s32[2,64,16,4]{1,3,2,0:T(4,128)} %param.7) | copy-start | bytes 98308
  0.6 2.9 %copy-start.2 = (s32[2,64,16,4]{1,3,2,0:T(4,128)S(1)}, s32[2,64,16,4]{1,3,2,0:T(4,128)}, u32[]{:S(2)}) copy-start(s32[2,64,16,4]{1,3,2,0:T(4,128)} %param.8) | copy-start | bytes 98308
  0.7 3.7 %copy-start.1 = (bf16[2,64,16,16]{1,3,2,0:T(8,128)(2,1)S(1)}, bf16[2,64,16,16]{1,3,2,0:T(8,128)(2,1)}, u32[]{:S(2)}) copy-start(bf16[2,64,16,16]{1,3,2,0:T(8,128)(2,1)} %param.9) | copy-start | bytes 196612
  0.7 1.5 %copy-start.4 = (f32[3072]{0:T(1024)S(1)}, f32[3072]{0:T(1024)}, u32[]{:S(2)}) copy-start(f32[3072]{0:T(1024)} %param.11) | copy-start | bytes 36868
  0.7 1.5 %copy-start.5 = (s32[1,10]{1,0:T(1,128)S(1)}, s32[1,10]{1,0:T(1,128)}, u32[]{:S(2)}) copy-start(s32[1,10]{1,0:T(1,128)} %param.12) | copy-start | bytes 124
  62.9 2.1 %copy-start = (bf16[48,64,256]{2,1,0:T(8,128)(2,1)}, bf16[48,64,256]{2,1,0:T(8,128)(2,1)S(1)}, u32[]{:S(2)}) copy-start(bf16[48,64,256]{2,1,0:T(8,128)(2,1)S(1)} %scatter_fusion) | copy-start | bytes 4718596

commit v3 on v2

--- a/solution.py
+++ b/solution.py
@@ -1,4 +1,5 @@
 import functools
+import math
 
 import jax
 import jax.numpy as jnp
@@ -27,14 +28,18 @@
     n,
     rows_ref,
     w_ref,
-    slab_ref,
+    touched_ref,
     state_ref,
+    table_ref,
     dither_ref,
     out_ref,
     state_out_ref,
     near,
     far,
     w_other,
+    table_in,
+    dither_in,
+    slab,
     slab_t,
     pooled_out,
     pooled_in,
@@ -59,9 +64,10 @@
     group = me // m
     local = lax.rem(me, m)
     mirror = lax.rem(me + m, n)
-    bags, samples = rows_ref.shape[2:]
-    slab_size = slab_ref.shape[0]
-    width = slab_t.shape[1]
+    samples = w_ref.shape[1]
+    bags = rows_ref.shape[3]
+    slab_size, width = slab.shape
+    touch_count = slab_size // BLOCK
     keeps = kept.shape[1] == m
     columns = pl.ds(pl.multiple_of(rep * width, width), width)
 
@@ -83,19 +89,28 @@
     def far_at(j):
         return (1 - group) * m + j
 
+    table_copy = pltpu.make_async_copy(table_ref.at[:, :, columns], table_in, small_sem.at[13])
+    table_copy.start()
+    own_rows = pltpu.make_async_copy(
+        rows_ref.at[:, :, local], near.at[rep, local], small_sem.at[0]
+    )
+    own_rows.start()
+    dither_copy = pltpu.make_async_copy(dither_ref.at[:, columns], dither_in, small_sem.at[14])
+    dither_copy.start()
     barrier = pltpu.get_barrier_semaphore()
     each(1, lambda j: pl.semaphore_signal(barrier, inc=1, **at(near_at(j))))
     each(0, lambda j: pl.semaphore_signal(barrier, inc=1, **at(far_at(j))))
     pl.semaphore_signal(barrier, inc=1, **partner)
-    slab_t[0] = slab_ref[:, columns].astype(jnp.float32).T.astype(jnp.bfloat16)
-    own_rows = pltpu.make_async_copy(rows_ref.at[local], near.at[rep, local], small_sem.at[0])
-    own_rows.start()
     total[...] = jnp.zeros_like(total)
+    table_copy.wait()
+    for block in range(touch_count):
+        slab[block * BLOCK : (block + 1) * BLOCK, :] = table_in[touched_ref[0, block]]
+    slab_t[0] = slab[...].astype(jnp.float32).T.astype(jnp.bfloat16)
     pl.semaphore_wait(barrier, n)
 
     def near_copy(j, slot):
         return pltpu.make_async_remote_copy(
-            rows_ref.at[j],
+            rows_ref.at[:, :, j],
             near.at[rep, slot],
             rows_send.at[0, j],
             near_recv.at[slot],
@@ -104,7 +119,7 @@
 
     def far_copy(j, slot):
         return pltpu.make_async_remote_copy(
-            rows_ref.at[j, 1 - group],
+            rows_ref.at[:, 1 - group, j],
             far.at[rep, slot],
             rows_send.at[1, j],
             far_recv.at[slot],
@@ -132,7 +147,8 @@
     offset_in_block = offset_in_block.astype(jnp.float32).astype(jnp.bfloat16)
     one = jnp.ones((BLOCK, samples), jnp.bfloat16)
 
-    def hits(rows):
+    def hits(micros):
+        rows = jnp.concatenate([micros[i] for i in range(micros.shape[0])], axis=-1)
         blocks = []
         block_of, offset_of = rows // BLOCK, lax.rem(rows, BLOCK)
         for block in range(slab_size // BLOCK):
@@ -168,7 +184,7 @@
         feature = me if which == 0 else mirror
 
         def pooled(j):
-            counted = hits(near[replica, j, table])
+            counted = hits(near[replica, j, :, table])
             if which == 0 and keeps:
                 kept[part, j] = counted
             return jnp.dot(slab_t[which], counted, preferred_element_type=jnp.float32).astype(
@@ -191,11 +207,14 @@
 
         def mixed(feature):
             def add(other, carry):
-                weight = weights[pl.ds(feature * n + other, 1), :]
+                weight = (
+                    weights[pl.ds(feature * n + other, 1), :]
+                    + weights[pl.ds(other * n + feature, 1), :]
+                )
                 return carry + weight * pooled_in[part, other].astype(jnp.float32)
 
-            zero = jnp.zeros((width, samples), jnp.float32)
-            return lax.fori_loop(0, n, add, zero, unroll=4).astype(jnp.bfloat16)
+            start = POOL_DECAY * pooled_in[part, feature].astype(jnp.float32)
+            return lax.fori_loop(0, n, add, start, unroll=4).astype(jnp.bfloat16)
 
         def send(peer):
             grad_out[part, peer] = mixed(peer)
@@ -215,7 +234,7 @@
             )
 
         def near_hits(j):
-            return kept[part, j] if keeps else hits(near[replica, j, group])
+            return kept[part, j] if keeps else hits(near[replica, j, :, group])
 
         def take_near(j):
             grad_copy(part, near_at(j), near_at(j)).wait_recv()
@@ -248,6 +267,12 @@
     swap_far.wait_recv()
     collect(1, 1 - rep)
 
+    pieces = []
+    for block in range(touch_count):
+        at_block = touched_ref[0, block]
+        pair = state_ref[pl.ds(at_block // 2, 1), :]
+        pieces.append(jnp.where(lax.rem(at_block, 2) == 0, pair[:, :BLOCK], pair[:, BLOCK:]))
+    state_row = jnp.concatenate(pieces, axis=1)
     grad = total[...]
     squares[0] = jnp.sum((grad * grad).T, axis=0, keepdims=True)
     square_copy = pltpu.make_async_remote_copy(
@@ -257,16 +282,24 @@
     square_copy.wait_recv()
     first = jnp.where(rep == 0, squares[0], squares[1])
     second = jnp.where(rep == 0, squares[1], squares[0])
-    state_next = state_ref[...] + (first + second) / (2.0 * width)
-    state_out_ref[...] = state_next
+    state_next = state_row + (first + second) / (2.0 * width)
     divisor = jnp.broadcast_to(jnp.sqrt(state_next) + 1e-08, (width, slab_size)).T
-    moved = slab_ref[:, columns].astype(jnp.float32) - LEARN_RATE * grad / divisor
-    rows_new[0] = dither_round(moved, dither_ref[:, columns])
+    moved = slab[...].astype(jnp.float32) - LEARN_RATE * grad / divisor
+    dither_copy.wait()
+    rows_new[0] = dither_round(moved, dither_in[...])
     new_copy = pltpu.make_async_remote_copy(
         rows_new.at[0], rows_new.at[1], small_sem.at[7], small_sem.at[8], **partner
     )
     new_copy.start()
     out_ref[:, columns] = rows_new[0]
+    state_all = state_ref[...]
+    block_at = 2 * lax.broadcasted_iota(jnp.int32, state_all.shape, 0)
+    block_at = block_at + lax.broadcasted_iota(jnp.int32, state_all.shape, 1) // BLOCK
+    for block in range(touch_count):
+        piece = state_next[:, block * BLOCK : (block + 1) * BLOCK]
+        piece = jnp.broadcast_to(jnp.concatenate([piece, piece], axis=1), state_all.shape)
+        state_all = jnp.where(block_at == touched_ref[0, block], piece, state_all)
+    state_out_ref[...] = state_all
 
     each(1, lambda j: near_copy(j, j).wait_send())
     each(0, lambda j: far_copy(j, j).wait_send())
@@ -284,27 +317,33 @@
     out_ref[:, pl.ds(pl.multiple_of((1 - rep) * width, width), width)] = rows_new[1]
 
 
-def fused_step(n, rows, weights, slab, state_row, dither):
-    bags, samples = rows.shape[2:]
-    slab_size, emb_width = slab.shape
+def fused_step(n, rows, weights, touched, state, table, dither):
+    micros, _, _, bags, _ = rows.shape
+    samples = weights.shape[1]
+    slab_size, emb_width = dither.shape
     width = emb_width // 2
     m = n // 2
     keep = m if 4 * m * slab_size * samples <= KEEP_BYTES else 1
     dma = pltpu.SemaphoreType.DMA
     block = (2, n, width, samples)
     vmem = pl.BlockSpec(memory_space=pltpu.VMEM)
+    smem = pl.BlockSpec(memory_space=pltpu.SMEM)
+    hbm = pl.BlockSpec(memory_space=pl.ANY)
     return pl.pallas_call(
         functools.partial(step_kernel, n),
         out_shape=(
             jax.ShapeDtypeStruct((slab_size, emb_width), jnp.bfloat16),
-            jax.ShapeDtypeStruct((1, slab_size), jnp.float32),
+            jax.ShapeDtypeStruct(state.shape, jnp.float32),
         ),
-        in_specs=[vmem] * 5,
+        in_specs=[vmem, vmem, smem, vmem, hbm, hbm],
         out_specs=(vmem, vmem),
         scratch_shapes=[
-            pltpu.VMEM((2, m, 2, bags, samples), jnp.int32),
-            pltpu.VMEM((2, m, bags, samples), jnp.int32),
+            pltpu.VMEM((2, m, micros, 2) + rows.shape[3:], jnp.int32),
+            pltpu.VMEM((2, m, micros) + rows.shape[3:], jnp.int32),
             pltpu.VMEM(weights.shape, jnp.float32),
+            pltpu.VMEM(table.shape[:2] + (width,), jnp.bfloat16),
+            pltpu.VMEM((slab_size, width), jnp.int32),
+            pltpu.VMEM((slab_size, width), jnp.bfloat16),
             pltpu.VMEM((2, width, slab_size), jnp.bfloat16),
             pltpu.VMEM((2, 2, m, width, samples), jnp.bfloat16),
             pltpu.VMEM(block, jnp.bfloat16),
@@ -314,7 +353,7 @@
             pltpu.VMEM((slab_size, width), jnp.float32),
             pltpu.VMEM((2, 1, slab_size), jnp.float32),
             pltpu.VMEM((2, slab_size, width), jnp.bfloat16),
-            dma((13,)),
+            dma((15,)),
             dma((2, m)),
             dma((m,)),
             dma((m,)),
@@ -325,7 +364,55 @@
         ],
         compiler_params=pltpu.CompilerParams(collective_id=0, has_side_effects=True),
         name="fused_step",
-    )(rows, weights, slab, state_row, dither)
+    )(rows, weights, touched, state, table, dither)
+
+
+def write_kernel(chunks, touched_ref, new_ref, table_ref, out_ref, held, read_sem, write_sem):
+    size = table_ref.shape[0] // chunks
+
+    def read(chunk):
+        part = pl.ds(chunk * size, size)
+        return pltpu.make_async_copy(table_ref.at[part], held.at[part], read_sem.at[chunk])
+
+    def write(chunk):
+        part = pl.ds(chunk * size, size)
+        return pltpu.make_async_copy(held.at[part], out_ref.at[part], write_sem.at[chunk])
+
+    for chunk in range(chunks):
+        read(chunk).start()
+    for chunk in range(chunks):
+        read(chunk).wait()
+        for block in range(touched_ref.shape[1]):
+            target = touched_ref[0, block]
+
+            @pl.when((target >= chunk * size) & (target < (chunk + 1) * size))
+            def _():
+                held[target] = new_ref[block]
+
+        write(chunk).start()
+    for chunk in range(chunks):
+        write(chunk).wait()
+
+
+def write_table(touched, new_rows, table):
+    chunks = math.gcd(table.shape[0], 4)
+    hbm = pl.BlockSpec(memory_space=pl.ANY)
+    return pl.pallas_call(
+        functools.partial(write_kernel, chunks),
+        out_shape=jax.ShapeDtypeStruct(table.shape, table.dtype),
+        in_specs=[
+            pl.BlockSpec(memory_space=pltpu.SMEM),
+            pl.BlockSpec(memory_space=pltpu.VMEM),
+            hbm,
+        ],
+        out_specs=hbm,
+        scratch_shapes=[
+            pltpu.VMEM(table.shape, table.dtype),
+            pltpu.SemaphoreType.DMA((chunks,)),
+            pltpu.SemaphoreType.DMA((chunks,)),
+        ],
+        name="write_table",
+    )(touched, new_rows, table)
 
 
 def per_device(
@@ -333,25 +420,21 @@
 ):
     micro_count, sample_count, feature_count, bag_count = lookup_block.shape
     n = lax.axis_size("mp")
-    samples = micro_count * sample_count
     row_count, emb_width = table.shape
     touch_count = touched_blocks.shape[1]
-    slab_size = touch_count * BLOCK
-    rows = (lookup_block * BLOCK + lookup_offset).reshape(samples, feature_count * bag_count)
-    rows = rows.T.reshape(2, feature_count // 2, bag_count, samples).swapaxes(0, 1)
-    cot = interaction_grad.reshape(samples, feature_count, feature_count).astype(jnp.float32)
-    weights = cot + jnp.swapaxes(cot, 1, 2) + POOL_DECAY * jnp.eye(feature_count)
-    weights = weights.reshape(samples, feature_count * feature_count).T
+    rows = (lookup_block * BLOCK + lookup_offset).transpose(0, 2, 3, 1)
+    rows = rows.reshape(micro_count, 2, feature_count // 2, bag_count, sample_count)
+    cot = interaction_grad.transpose(2, 3, 0, 1).astype(jnp.float32)
+    cot = cot.reshape(feature_count * feature_count, micro_count * sample_count)
     table_blocks = table.reshape(row_count // BLOCK, BLOCK, emb_width)
-    slab = table_blocks[touched_blocks[0]].reshape(slab_size, emb_width)
-    state_blocks = adagrad_state.reshape(row_count // BLOCK, BLOCK)
-    state_row = state_blocks[touched_blocks[0]].reshape(1, slab_size)
-    new_rows, state_next = fused_step(n, rows, weights, slab, state_row, dither[0])
-    updated_blocks = table_blocks.at[touched_blocks[0]].set(
-        new_rows.reshape(touch_count, BLOCK, emb_width)
-    )
-    updated_state = state_blocks.at[touched_blocks[0]].set(state_next.reshape(touch_count, BLOCK))
-    return (updated_blocks.reshape(row_count, emb_width), updated_state.reshape(row_count))
+    state = adagrad_state.reshape(row_count // (2 * BLOCK), 2 * BLOCK)
+    new_rows, new_state = fused_step(
+        n, rows, cot, touched_blocks, state, table_blocks, dither[0]
+    )
+    new_table = write_table(
+        touched_blocks, new_rows.reshape(touch_count, BLOCK, emb_width), table_blocks
+    )
+    return (new_table.reshape(row_count, emb_width), new_state.reshape(row_count))
 
 
 def solution(mesh):

time: 65.3 us -> 64.5 us (0.988)
  local copies, waits for them, and re-layouts: 8.46 us -> 1.65 us
  Pallas kernels: 54.3 us -> 59.5 us
  other arithmetic: 1.47 us -> 2.44 us
    pallas_call x0 -> x1, Pallas kernels: none -> 3.25 us  [write_table(): pl.pallas_call(functools.partial(write_kernel, chunks), out_shape=jax.Sha...]
    scatter x2 -> x0, local copies, waits for them, and re-layouts: 2.52 us -> none  [the longest x1 1.89 us: per_device(): table_blocks.at[touched_blocks[0]]]
    pallas_call x1, Pallas kernels: 54.3 us -> 56.3 us  [fused_step(): pl.pallas_call(functools.partial(step_kernel, n), out_shape=(jax.ShapeDty...]
    gather x2 -> x0, local copies, waits for them, and re-layouts: 1.86 us -> none  [the longest x1 1.31 us: per_device(): slab = table_blocks[touched_blocks[0]].reshape(slab_size, emb_width)]
    reshape x6 -> x2, local copies, waits for them, and re-layouts: 2.18 us -> 1.05 us  [per_device(): cot = cot.reshape(feature_count * feature_count, micro_count * sample_count)]
    reshape x0 -> x1, other arithmetic: none -> 0.92 us  [per_device(): cot = cot.reshape(feature_count * feature_count, micro_count * sample_count)]
    unnamed x13 -> x3, local copies, waits for them, and re-layouts: 1.52 us -> 0.61 us
    add x2 -> x1, other arithmetic: 0.77 us -> 1.52 us  [per_device(): rows = (lookup_block * BLOCK + lookup_offset).transpose(0, 2, 3, 1)]
where the time goes in v3:
time: 64.5 us; the launch traced here: 64.3 us
  Pallas kernels  59.5 us (92%)
  other arithmetic  2.44 us (4%)
  local copies, waits for them, and re-layouts  1.65 us (3%)
  between operations  0.67 us (1%)
    pallas_call x1, Pallas kernels, fused_step(): pl.pallas_call(functools.partial(step_kernel, n), out_shape=(jax.ShapeDty...  56.3 us
    pallas_call x1, Pallas kernels, write_table(): pl.pallas_call(functools.partial(write_kernel, chunks), out_shape=jax.Sha...  3.25 us
    add x1, other arithmetic, per_device(): rows = (lookup_block * BLOCK + lookup_offset).transpose(0, 2, 3, 1)  1.52 us

profile of v3, /device:TPU:0, one launch (start us, length us, event | category | flops | bytes accessed | tf_op | source)
XLA Modules:
  0.0 64.3 jit_solution(288161943185823295)
XLA Ops:
  0.6 1.5 %multiply_add_fusion = s32[2,64,16,4]{1,3,2,0:T(4,128)} fusion(s32[2,64,16,4]{1,3,2,0:T(4,128)} %param.8, s32[2,64,16,4]{1,3,2,0:T(4,128)} %param.7), kind=kLoop, calls=%fused_computation.1 | loop fusion | flops 16384 | bytes 98304 | tf_op jit(solution)/shard_map/add | solution.py:425
  2.1 0.9 %convert_bitcast_fusion = f32[16,16,2,64]{3,1,0,2:T(8,128)S(1)} fusion(bf16[2,64,16,16]{1,3,2,0:T(8,128)(2,1)} %param.9), kind=kLoop, calls=%fused_computation | loop fusion | flops 32768 | bytes 196608 | tf_op jit(solution)/shard_map/reshape | solution.py:428
  3.1 0.2 copy.9
  3.3 0.8 %reshape.36.w_ref = f32[256,128]{1,0:T(8,128)} reshape(f32[16,16,2,64]{3,2,1,0:T(2,128)S(1)} %copy.9) | data formatting | bytes 262144 | tf_op jit(solution)/shard_map/reshape | solution.py:428
  4.1 56.3 %fused_step.1 = (bf16[640,256]{1,0:T(8,128)(2,1)}, f32[24,128]{1,0:T(8,128)}) custom-call(s32[2,2,8,4,64]{4,3,2,1,0:T(4,128)} %bitcast.16, f32[256,128]{1,0:T(8,128)} %reshape.36.w_ref, s32[1,10]{1,0:T(1,128)} %touched_ref.3, f32[24,128]{1,0:T(8,128)} %bitcast.17, bf16[48,64,256]{2,1,0:T(8,128)(2,1)} %bitcast.11, s32[640,256]{1,0:T(8,128)} %bitcast.14), custom_call_target="tpu_custom_call" | custom-call | tf_op jit(solution)/shard_map/fused_step/pallas_call | solution.py:332
  60.4 0.0 copy-start
  60.4 3.3 %write_table.1 = bf16[48,64,256]{2,1,0:T(8,128)(2,1)} custom-call(s32[1,10]{1,0:T(1,128)} %touched_ref.3, bf16[10,64,256]{2,1,0:T(8,128)(2,1)} %bitcast.15, bf16[48,64,256]{2,1,0:T(8,128)(2,1)} %bitcast.12), custom_call_target="tpu_custom_call" | custom-call | tf_op jit(solution)/shard_map/write_table/pallas_call | solution.py:400
  63.7 0.0 copy-done
  63.7 0.6 copy.11
Async XLA Ops:
  60.4 3.3 %copy-start = (f32[24,128]{1,0:T(8,128)S(1)}, f32[24,128]{1,0:T(8,128)}, u32[]{:S(2)}) copy-start(f32[24,128]{1,0:T(8,128)} %get-tuple-element.5) | copy-start | bytes 36868

commit v4 on v3

--- a/solution.py
+++ b/solution.py
@@ -26,16 +26,23 @@
 
 def step_kernel(
     n,
-    rows_ref,
-    w_ref,
+    block_hbm,
+    offset_hbm,
+    cot_ref,
     touched_ref,
-    state_ref,
+    state_hbm,
     table_ref,
     dither_ref,
     out_ref,
     state_out_ref,
+    block_ref,
+    offset_ref,
+    state_ref,
+    rows_ref,
+    cot_in,
     near,
     far,
+    w_ref,
     w_other,
     table_in,
     dither_in,
@@ -89,18 +96,24 @@
     def far_at(j):
         return (1 - group) * m + j
 
-    table_copy = pltpu.make_async_copy(table_ref.at[:, :, columns], table_in, small_sem.at[13])
-    table_copy.start()
-    own_rows = pltpu.make_async_copy(
-        rows_ref.at[:, :, local], near.at[rep, local], small_sem.at[0]
-    )
-    own_rows.start()
-    dither_copy = pltpu.make_async_copy(dither_ref.at[:, columns], dither_in, small_sem.at[14])
-    dither_copy.start()
     barrier = pltpu.get_barrier_semaphore()
     each(1, lambda j: pl.semaphore_signal(barrier, inc=1, **at(near_at(j))))
     each(0, lambda j: pl.semaphore_signal(barrier, inc=1, **at(far_at(j))))
     pl.semaphore_signal(barrier, inc=1, **partner)
+    block_copy = pltpu.make_async_copy(block_hbm, block_ref, small_sem.at[17])
+    block_copy.start()
+    offset_copy = pltpu.make_async_copy(offset_hbm, offset_ref, small_sem.at[18])
+    offset_copy.start()
+    state_copy = pltpu.make_async_copy(state_hbm, state_ref, small_sem.at[19])
+    state_copy.start()
+    table_copy = pltpu.make_async_copy(table_ref.at[:, :, columns], table_in, small_sem.at[13])
+    table_copy.start()
+    dither_copy = pltpu.make_async_copy(dither_ref.at[:, columns], dither_in, small_sem.at[14])
+    dither_copy.start()
+    block_copy.wait()
+    offset_copy.wait()
+    rows_ref[...] = block_ref[...] * BLOCK + offset_ref[...]
+    near[rep, local] = rows_ref[:, :, local]
     total[...] = jnp.zeros_like(total)
     table_copy.wait()
     for block in range(touch_count):
@@ -131,12 +144,26 @@
         slab_t.at[0], slab_t.at[1], small_sem.at[9], small_sem.at[10], **at(mirror)
     )
     slab_copy.start()
+    each(0, lambda j: far_copy(j, local).start())
+    cot_size = cot_in.shape[1]
+
+    def spread(chunk, carry):
+        cot_copy = pltpu.make_async_copy(
+            cot_ref.at[:, pl.ds(chunk * cot_size, cot_size)], cot_in, small_sem.at[0]
+        )
+        cot_copy.start()
+        cot_copy.wait()
+        for i in range(cot_size):
+            pieces = [cot_in[micro, i].astype(jnp.float32) for micro in range(cot_in.shape[0])]
+            at_row = pl.multiple_of((chunk * cot_size + i) * n, n)
+            w_ref[pl.ds(at_row, n), :] = jnp.concatenate(pieces, axis=-1)
+        return carry
+
+    lax.fori_loop(0, n // cot_size, spread, 0)
     w_copy = pltpu.make_async_remote_copy(
         w_ref, w_other, small_sem.at[1], small_sem.at[2], **partner
     )
     w_copy.start()
-    each(0, lambda j: far_copy(j, local).start())
-    own_rows.wait()
     each(1, lambda j: near_copy(j, j).wait_recv())
     swap_near = pltpu.make_async_remote_copy(
         near.at[rep], near.at[rep], small_sem.at[3], small_sem.at[4], **partner
@@ -267,6 +294,7 @@
     swap_far.wait_recv()
     collect(1, 1 - rep)
 
+    state_copy.wait()
     pieces = []
     for block in range(touch_count):
         at_block = touched_ref[0, block]
@@ -284,13 +312,23 @@
     second = jnp.where(rep == 0, squares[1], squares[0])
     state_next = state_row + (first + second) / (2.0 * width)
     divisor = jnp.broadcast_to(jnp.sqrt(state_next) + 1e-08, (width, slab_size)).T
-    moved = slab[...].astype(jnp.float32) - LEARN_RATE * grad / divisor
     dither_copy.wait()
-    rows_new[0] = dither_round(moved, dither_in[...])
-    new_copy = pltpu.make_async_remote_copy(
-        rows_new.at[0], rows_new.at[1], small_sem.at[7], small_sem.at[8], **partner
-    )
-    new_copy.start()
+    size = slab_size // 2
+    new_copies = []
+    for piece in range(2):
+        part = pl.ds(piece * size, size)
+        span = slice(piece * size, (piece + 1) * size)
+        moved = slab[span, :].astype(jnp.float32) - LEARN_RATE * total[span, :] / divisor[span]
+        rows_new[0, span] = dither_round(moved, dither_in[span, :])
+        new_copy = pltpu.make_async_remote_copy(
+            rows_new.at[0, part],
+            rows_new.at[1, part],
+            small_sem.at[7 + 8 * piece],
+            small_sem.at[8 + 8 * piece],
+            **partner,
+        )
+        new_copy.start()
+        new_copies.append(new_copy)
     out_ref[:, columns] = rows_new[0]
     state_all = state_ref[...]
     block_at = 2 * lax.broadcasted_iota(jnp.int32, state_all.shape, 0)
@@ -313,13 +351,15 @@
     swap_near.wait_send()
     swap_far.wait_send()
     square_copy.wait_send()
-    new_copy.wait()
+    for new_copy in new_copies:
+        new_copy.wait()
     out_ref[:, pl.ds(pl.multiple_of((1 - rep) * width, width), width)] = rows_new[1]
 
 
-def fused_step(n, rows, weights, touched, state, table, dither):
-    micros, _, _, bags, _ = rows.shape
-    samples = weights.shape[1]
+def fused_step(n, blocks, offsets, cot, touched, state, table, dither):
+    micros, sample_count = blocks.shape[0], blocks.shape[-1]
+    samples = micros * sample_count
+    cot_size = math.gcd(n, 16)
     slab_size, emb_width = dither.shape
     width = emb_width // 2
     m = n // 2
@@ -328,19 +368,25 @@
     block = (2, n, width, samples)
     vmem = pl.BlockSpec(memory_space=pltpu.VMEM)
     smem = pl.BlockSpec(memory_space=pltpu.SMEM)
-    hbm = pl.BlockSpec(memory_space=pl.ANY)
+    hbm = pl.BlockSpec(memory_space=pltpu.HBM)
     return pl.pallas_call(
         functools.partial(step_kernel, n),
         out_shape=(
             jax.ShapeDtypeStruct((slab_size, emb_width), jnp.bfloat16),
             jax.ShapeDtypeStruct(state.shape, jnp.float32),
         ),
-        in_specs=[vmem, vmem, smem, vmem, hbm, hbm],
+        in_specs=[hbm, hbm, hbm, smem, hbm, hbm, hbm],
         out_specs=(vmem, vmem),
         scratch_shapes=[
-            pltpu.VMEM((2, m, micros, 2) + rows.shape[3:], jnp.int32),
-            pltpu.VMEM((2, m, micros) + rows.shape[3:], jnp.int32),
-            pltpu.VMEM(weights.shape, jnp.float32),
+            pltpu.VMEM(blocks.shape, jnp.int32),
+            pltpu.VMEM(blocks.shape, jnp.int32),
+            pltpu.VMEM(state.shape, jnp.float32),
+            pltpu.VMEM(blocks.shape, jnp.int32),
+            pltpu.VMEM((micros, cot_size, n, sample_count), jnp.bfloat16),
+            pltpu.VMEM((2, m, micros, 2) + blocks.shape[3:], jnp.int32),
+            pltpu.VMEM((2, m, micros) + blocks.shape[3:], jnp.int32),
+            pltpu.VMEM((n * n, samples), jnp.float32),
+            pltpu.VMEM((n * n, samples), jnp.float32),
             pltpu.VMEM(table.shape[:2] + (width,), jnp.bfloat16),
             pltpu.VMEM((slab_size, width), jnp.int32),
             pltpu.VMEM((slab_size, width), jnp.bfloat16),
@@ -353,7 +399,7 @@
             pltpu.VMEM((slab_size, width), jnp.float32),
             pltpu.VMEM((2, 1, slab_size), jnp.float32),
             pltpu.VMEM((2, slab_size, width), jnp.bfloat16),
-            dma((15,)),
+            dma((20,)),
             dma((2, m)),
             dma((m,)),
             dma((m,)),
@@ -364,55 +410,44 @@
         ],
         compiler_params=pltpu.CompilerParams(collective_id=0, has_side_effects=True),
         name="fused_step",
-    )(rows, weights, touched, state, table, dither)
-
-
-def write_kernel(chunks, touched_ref, new_ref, table_ref, out_ref, held, read_sem, write_sem):
-    size = table_ref.shape[0] // chunks
-
-    def read(chunk):
-        part = pl.ds(chunk * size, size)
-        return pltpu.make_async_copy(table_ref.at[part], held.at[part], read_sem.at[chunk])
-
-    def write(chunk):
-        part = pl.ds(chunk * size, size)
-        return pltpu.make_async_copy(held.at[part], out_ref.at[part], write_sem.at[chunk])
-
-    for chunk in range(chunks):
-        read(chunk).start()
-    for chunk in range(chunks):
-        read(chunk).wait()
-        for block in range(touched_ref.shape[1]):
-            target = touched_ref[0, block]
-
-            @pl.when((target >= chunk * size) & (target < (chunk + 1) * size))
-            def _():
-                held[target] = new_ref[block]
-
-        write(chunk).start()
-    for chunk in range(chunks):
-        write(chunk).wait()
-
-
-def write_table(touched, new_rows, table):
-    chunks = math.gcd(table.shape[0], 4)
-    hbm = pl.BlockSpec(memory_space=pl.ANY)
+    )(blocks, offsets, cot, touched, state, table, dither)
+
+
+def write_kernel(touched_ref, new_ref, state_ref, table_ref, out_ref, state_out_ref, sem):
+    state_out_ref[...] = state_ref[...]
+
+    def write(block, carry):
+        new = -1
+        for i in range(touched_ref.shape[1]):
+            new = jnp.where(touched_ref[0, i] == block, i, new)
+
+        @pl.when(new >= 0)
+        def _():
+            pltpu.make_async_copy(new_ref.at[new], out_ref.at[block], sem).start()
+
+        @pl.when(new < 0)
+        def _():
+            pltpu.make_async_copy(table_ref.at[block], out_ref.at[block], sem).start()
+
+        return carry
+
+    lax.fori_loop(0, table_ref.shape[0], write, 0)
+    pltpu.make_async_copy(table_ref, out_ref, sem).wait()
+
+
+def write_table(touched, new_rows, state, table):
+    vmem = pl.BlockSpec(memory_space=pltpu.VMEM)
     return pl.pallas_call(
-        functools.partial(write_kernel, chunks),
-        out_shape=jax.ShapeDtypeStruct(table.shape, table.dtype),
-        in_specs=[
-            pl.BlockSpec(memory_space=pltpu.SMEM),
-            pl.BlockSpec(memory_space=pltpu.VMEM),
-            hbm,
-        ],
-        out_specs=hbm,
-        scratch_shapes=[
-            pltpu.VMEM(table.shape, table.dtype),
-            pltpu.SemaphoreType.DMA((chunks,)),
-            pltpu.SemaphoreType.DMA((chunks,)),
-        ],
+        write_kernel,
+        out_shape=(
+            jax.ShapeDtypeStruct(table.shape, table.dtype),
+            jax.ShapeDtypeStruct(state.shape, state.dtype),
+        ),
+        in_specs=[pl.BlockSpec(memory_space=pltpu.SMEM), vmem, vmem, vmem],
+        out_specs=(pl.BlockSpec(memory_space=pl.ANY), vmem),
+        scratch_shapes=[pltpu.SemaphoreType.DMA],
         name="write_table",
-    )(touched, new_rows, table)
+    )(touched, new_rows, state, table)
 
 
 def per_device(
@@ -422,18 +457,17 @@
     n = lax.axis_size("mp")
     row_count, emb_width = table.shape
     touch_count = touched_blocks.shape[1]
-    rows = (lookup_block * BLOCK + lookup_offset).transpose(0, 2, 3, 1)
-    rows = rows.reshape(micro_count, 2, feature_count // 2, bag_count, sample_count)
-    cot = interaction_grad.transpose(2, 3, 0, 1).astype(jnp.float32)
-    cot = cot.reshape(feature_count * feature_count, micro_count * sample_count)
+    split = (micro_count, 2, feature_count // 2, bag_count, sample_count)
+    blocks = lookup_block.transpose(0, 2, 3, 1).reshape(split)
+    offsets = lookup_offset.transpose(0, 2, 3, 1).reshape(split)
+    cot = interaction_grad.transpose(0, 2, 3, 1)
     table_blocks = table.reshape(row_count // BLOCK, BLOCK, emb_width)
     state = adagrad_state.reshape(row_count // (2 * BLOCK), 2 * BLOCK)
     new_rows, new_state = fused_step(
-        n, rows, cot, touched_blocks, state, table_blocks, dither[0]
-    )
-    new_table = write_table(
-        touched_blocks, new_rows.reshape(touch_count, BLOCK, emb_width), table_blocks
-    )
+        n, blocks, offsets, cot, touched_blocks, state, table_blocks, dither[0]
+    )
+    new_rows = new_rows.reshape(touch_count, BLOCK, emb_width)
+    new_table, new_state = write_table(touched_blocks, new_rows, new_state, table_blocks)
     return (new_table.reshape(row_count, emb_width), new_state.reshape(row_count))
 
 

time: 64.5 us -> 60.4 us (0.936)
  other arithmetic: 2.44 us -> 0 us
  local copies, waits for them, and re-layouts: 1.65 us -> 0 us
    add x1 -> x0, other arithmetic: 1.52 us -> none  [per_device(): rows = (lookup_block * BLOCK + lookup_offset).transpose(0, 2, 3, 1)]
    reshape x2 -> x0, local copies, waits for them, and re-layouts: 1.05 us -> none  [per_device(): cot = cot.reshape(feature_count * feature_count, micro_count * sample_count)]
    reshape x1 -> x0, other arithmetic: 0.92 us -> none  [per_device(): cot = cot.reshape(feature_count * feature_count, micro_count * sample_count)]
where the time goes in v4:
time: 60.4 us; the launch traced here: 60.2 us
  Pallas kernels  59.6 us (99%)
  between operations  0.64 us (1%)
    pallas_call x1, Pallas kernels, fused_step(): pl.pallas_call(functools.partial(step_kernel, n), out_shape=(jax.ShapeDty...  56.1 us
    pallas_call x1, Pallas kernels, write_table(): pl.pallas_call(write_kernel, out_shape=(jax.ShapeDtypeStruct(table.shape,...  3.47 us

profile of v4, /device:TPU:0, one launch (start us, length us, event | category | flops | bytes accessed | tf_op | source)
XLA Modules:
  0.0 60.2 jit_solution(6849131697427011624)
XLA Ops:
  0.6 56.1 %fused_step.1 = (bf16[640,256]{1,0:T(8,128)(2,1)}, f32[24,128]{1,0:T(8,128)}) custom-call(s32[2,2,8,4,64]{4,3,2,1,0:T(4,128)} %bitcast.18, s32[2,2,8,4,64]{4,3,2,1,0:T(4,128)} %bitcast.19, bf16[2,16,16,64]{3,2,1,0:T(8,128)(2,1)} %bitcast.17, s32[1,10]{1,0:T(1,128)} %touched_ref.3, f32[24,128]{1,0:T(8,128)} %bitcast.20, bf16[48,64,256]{2,1,0:T(8,128)(2,1)} %bitcast.13, ...), custom_call_target="tpu_custom_call" | custom-call | tf_op jit(solution)/shard_map/fused_step/pallas_call | solution.py:372
  56.8 3.5 %write_table.1 = (bf16[48,64,256]{2,1,0:T(8,128)(2,1)}, f32[24,128]{1,0:T(8,128)}) custom-call(s32[1,10]{1,0:T(1,128)} %touched_ref.3, bf16[10,64,256]{2,1,0:T(8,128)(2,1)} %bitcast.16, f32[24,128]{1,0:T(8,128)} %get-tuple-element.7.state_ref, bf16[48,64,256]{2,1,0:T(8,128)(2,1)} %bitcast.14), custom_call_target="tpu_custom_call" | custom-call | tf_op jit(solution)/shard_map/write_table/pallas_call | solution.py:440

commit v5 on v4

--- a/solution.py
+++ b/solution.py
@@ -75,7 +75,7 @@
     bags = rows_ref.shape[3]
     slab_size, width = slab.shape
     touch_count = slab_size // BLOCK
-    keeps = kept.shape[1] == m
+    keeps = kept.shape[2] == m
     columns = pl.ds(pl.multiple_of(rep * width, width), width)
 
     def at(peer):
@@ -211,9 +211,12 @@
         feature = me if which == 0 else mirror
 
         def pooled(j):
-            counted = hits(near[replica, j, :, table])
-            if which == 0 and keeps:
-                kept[part, j] = counted
+            if which == 1 and keeps:
+                counted = kept[1, part, j]
+            else:
+                counted = hits(near[replica, j, :, table])
+                if keeps:
+                    kept[0, part, j] = counted
             return jnp.dot(slab_t[which], counted, preferred_element_type=jnp.float32).astype(
                 jnp.bfloat16
             )
@@ -261,7 +264,7 @@
             )
 
         def near_hits(j):
-            return kept[part, j] if keeps else hits(near[replica, j, :, group])
+            return kept[0, part, j] if keeps else hits(near[replica, j, :, group])
 
         def take_near(j):
             grad_copy(part, near_at(j), near_at(j)).wait_recv()
@@ -284,6 +287,16 @@
         far.at[rep], far.at[rep], small_sem.at[11], small_sem.at[12], **partner
     )
     swap_far.start()
+
+    def keep_mirror(part, replica):
+        def keep_one(j):
+            kept[1, part, j] = hits(near[replica, j, :, 1 - group])
+
+        each(0, keep_one)
+
+    if keeps:
+        keep_mirror(0, rep)
+        keep_mirror(1, 1 - rep)
     slab_copy.wait_recv()
     pool(0, rep, 1)
     pool(1, 1 - rep, 1)
@@ -363,7 +376,7 @@
     slab_size, emb_width = dither.shape
     width = emb_width // 2
     m = n // 2
-    keep = m if 4 * m * slab_size * samples <= KEEP_BYTES else 1
+    keep = m if 8 * m * slab_size * samples <= KEEP_BYTES else 1
     dma = pltpu.SemaphoreType.DMA
     block = (2, n, width, samples)
     vmem = pl.BlockSpec(memory_space=pltpu.VMEM)
@@ -395,7 +408,7 @@
             pltpu.VMEM(block, jnp.bfloat16),
             pltpu.VMEM(block, jnp.bfloat16),
             pltpu.VMEM(block, jnp.bfloat16),
-            pltpu.VMEM((2, keep, slab_size, samples), jnp.bfloat16),
+            pltpu.VMEM((2, 2, keep, slab_size, samples), jnp.bfloat16),
             pltpu.VMEM((slab_size, width), jnp.float32),
             pltpu.VMEM((2, 1, slab_size), jnp.float32),
             pltpu.VMEM((2, slab_size, width), jnp.bfloat16),
@@ -413,39 +426,49 @@
     )(blocks, offsets, cot, touched, state, table, dither)
 
 
-def write_kernel(touched_ref, new_ref, state_ref, table_ref, out_ref, state_out_ref, sem):
+def write_kernel(
+    chunks, touched_ref, new_ref, state_ref, table_ref, out_ref, state_out_ref, held, read, write
+):
+    size = table_ref.shape[0] // chunks
+    parts = [pl.ds(chunk * size, size) for chunk in range(chunks)]
+    reads = [
+        pltpu.make_async_copy(table_ref.at[part], held.at[part], read.at[chunk])
+        for chunk, part in enumerate(parts)
+    ]
+    writes = [
+        pltpu.make_async_copy(held.at[part], out_ref.at[part], write.at[chunk])
+        for chunk, part in enumerate(parts)
+    ]
+    for copy in reads:
+        copy.start()
     state_out_ref[...] = state_ref[...]
-
-    def write(block, carry):
-        new = -1
-        for i in range(touched_ref.shape[1]):
-            new = jnp.where(touched_ref[0, i] == block, i, new)
-
-        @pl.when(new >= 0)
-        def _():
-            pltpu.make_async_copy(new_ref.at[new], out_ref.at[block], sem).start()
-
-        @pl.when(new < 0)
-        def _():
-            pltpu.make_async_copy(table_ref.at[block], out_ref.at[block], sem).start()
-
-        return carry
-
-    lax.fori_loop(0, table_ref.shape[0], write, 0)
-    pltpu.make_async_copy(table_ref, out_ref, sem).wait()
+    for copy in reads:
+        copy.wait()
+    for block in range(touched_ref.shape[1]):
+        held[touched_ref[0, block]] = new_ref[block]
+    for copy in writes:
+        copy.start()
+    for copy in writes:
+        copy.wait()
 
 
 def write_table(touched, new_rows, state, table):
+    chunks = math.gcd(table.shape[0], 4)
+    hbm = pl.BlockSpec(memory_space=pl.ANY)
     vmem = pl.BlockSpec(memory_space=pltpu.VMEM)
     return pl.pallas_call(
-        write_kernel,
+        functools.partial(write_kernel, chunks),
         out_shape=(
             jax.ShapeDtypeStruct(table.shape, table.dtype),
             jax.ShapeDtypeStruct(state.shape, state.dtype),
         ),
-        in_specs=[pl.BlockSpec(memory_space=pltpu.SMEM), vmem, vmem, vmem],
-        out_specs=(pl.BlockSpec(memory_space=pl.ANY), vmem),
-        scratch_shapes=[pltpu.SemaphoreType.DMA],
+        in_specs=[pl.BlockSpec(memory_space=pltpu.SMEM), vmem, vmem, hbm],
+        out_specs=(hbm, vmem),
+        scratch_shapes=[
+            pltpu.VMEM(table.shape, table.dtype),
+            pltpu.SemaphoreType.DMA((chunks,)),
+            pltpu.SemaphoreType.DMA((chunks,)),
+        ],
         name="write_table",
     )(touched, new_rows, state, table)
 

time: 60.4 us -> 63.3 us (1.048)
  Pallas kernels: 59.6 us -> 62.4 us
    pallas_call x1, Pallas kernels: 56.1 us -> 58.2 us  [fused_step(): pl.pallas_call(functools.partial(step_kernel, n), out_shape=(jax.ShapeDty...]
    pallas_call x1, Pallas kernels: 3.47 us -> 4.16 us  [write_table(): pl.pallas_call(functools.partial(write_kernel, chunks), out_shape=(jax.Sh...]
where the time goes in v5:
time: 63.3 us; the launch traced here: 63 us
  Pallas kernels  62.4 us (99%)
  between operations  0.64 us (1%)
    pallas_call x1, Pallas kernels, fused_step(): pl.pallas_call(functools.partial(step_kernel, n), out_shape=(jax.ShapeDty...  58.2 us
    pallas_call x1, Pallas kernels, write_table(): pl.pallas_call(functools.partial(write_kernel, chunks), out_shape=(jax.Sh...  4.16 us

profile of v5, /device:TPU:0, one launch (start us, length us, event | category | flops | bytes accessed | tf_op | source)
XLA Modules:
  0.0 63.0 jit_solution(17249157155076448837)
XLA Ops:
  0.6 58.2 %fused_step.1 = (bf16[640,256]{1,0:T(8,128)(2,1)}, f32[24,128]{1,0:T(8,128)}) custom-call(s32[2,2,8,4,64]{4,3,2,1,0:T(4,128)} %bitcast.18, s32[2,2,8,4,64]{4,3,2,1,0:T(4,128)} %bitcast.19, bf16[2,16,16,64]{3,2,1,0:T(8,128)(2,1)} %bitcast.17, s32[1,10]{1,0:T(1,128)} %touched_ref.3, f32[24,128]{1,0:T(8,128)} %bitcast.20, bf16[48,64,256]{2,1,0:T(8,128)(2,1)} %bitcast.13, ...), custom_call_target="tpu_custom_call" | custom-call | tf_op jit(solution)/shard_map/fused_step/pallas_call | solution.py:385
  58.9 4.2 %write_table.1 = (bf16[48,64,256]{2,1,0:T(8,128)(2,1)}, f32[24,128]{1,0:T(8,128)}) custom-call(s32[1,10]{1,0:T(1,128)} %touched_ref.3, bf16[10,64,256]{2,1,0:T(8,128)(2,1)} %bitcast.16, f32[24,128]{1,0:T(8,128)} %get-tuple-element.7.state_ref, bf16[48,64,256]{2,1,0:T(8,128)(2,1)} %bitcast.14), custom_call_target="tpu_custom_call" | custom-call | tf_op jit(solution)/shard_map/write_table/pallas_call | solution.py:459

commit v6 on v4

--- a/solution.py
+++ b/solution.py
@@ -277,17 +277,17 @@
         each(0, take_far)
 
     pool(0, rep, 0)
+    slab_copy.wait_recv()
+    pool(0, rep, 1)
     swap_near.wait_recv()
     pool(1, 1 - rep, 0)
+    interact(0, w_ref)
+    pool(1, 1 - rep, 1)
     each(0, lambda j: far_copy(j, j).wait_recv())
     swap_far = pltpu.make_async_remote_copy(
         far.at[rep], far.at[rep], small_sem.at[11], small_sem.at[12], **partner
     )
     swap_far.start()
-    slab_copy.wait_recv()
-    pool(0, rep, 1)
-    pool(1, 1 - rep, 1)
-    interact(0, w_ref)
     w_copy.wait_recv()
     interact(1, w_other)
     collect(0, rep)

time: 60.4 us -> 59.6 us (0.987)
  Pallas kernels: 59.6 us -> 58.8 us
    pallas_call x1, Pallas kernels: 56.1 us -> 55.3 us  [fused_step(): pl.pallas_call(functools.partial(step_kernel, n), out_shape=(jax.ShapeDty...]
where the time goes in v6:
time: 59.6 us; the launch traced here: 59.4 us
  Pallas kernels  58.8 us (99%)
  between operations  0.64 us (1%)
    pallas_call x1, Pallas kernels, fused_step(): pl.pallas_call(functools.partial(step_kernel, n), out_shape=(jax.ShapeDty...  55.3 us
    pallas_call x1, Pallas kernels, write_table(): pl.pallas_call(write_kernel, out_shape=(jax.ShapeDtypeStruct(table.shape,...  3.47 us

profile of v6, /device:TPU:0, one launch (start us, length us, event | category | flops | bytes accessed | tf_op | source)
XLA Modules:
  0.0 59.4 jit_solution(5475789017468357700)
XLA Ops:
  0.6 55.3 %fused_step.1 = (bf16[640,256]{1,0:T(8,128)(2,1)}, f32[24,128]{1,0:T(8,128)}) custom-call(s32[2,2,8,4,64]{4,3,2,1,0:T(4,128)} %bitcast.18, s32[2,2,8,4,64]{4,3,2,1,0:T(4,128)} %bitcast.19, bf16[2,16,16,64]{3,2,1,0:T(8,128)(2,1)} %bitcast.17, s32[1,10]{1,0:T(1,128)} %touched_ref.3, f32[24,128]{1,0:T(8,128)} %bitcast.20, bf16[48,64,256]{2,1,0:T(8,128)(2,1)} %bitcast.13, ...), custom_call_target="tpu_custom_call" | custom-call | tf_op jit(solution)/shard_map/fused_step/pallas_call | solution.py:372
  55.9 3.5 %write_table.1 = (bf16[48,64,256]{2,1,0:T(8,128)(2,1)}, f32[24,128]{1,0:T(8,128)}) custom-call(s32[1,10]{1,0:T(1,128)} %touched_ref.3, bf16[10,64,256]{2,1,0:T(8,128)(2,1)} %bitcast.16, f32[24,128]{1,0:T(8,128)} %get-tuple-element.7.state_ref, bf16[48,64,256]{2,1,0:T(8,128)(2,1)} %bitcast.14), custom_call_target="tpu_custom_call" | custom-call | tf_op jit(solution)/shard_map/write_table/pallas_call | solution.py:440
